TPU v7x, 32 devices: a whole 2x2x4 slice. The times are simulated.
32 devices in a mesh: dp: 4 (over z), ctx: 4 (over y, x), tensor: 2 (over core).
Axes of the slice: x: 2, y: 2, z: 4, core: 2. Of those that a mesh axis runs over, the one named last changes fastest.
Arguments:
- tokens: bfloat16 [4096, 1024], P(('dp', 'ctx')), may hold values from -6 to 6
- doc_lengths: int32 [4, 8], P('dp'), may hold values from 1 to 512, 1024 in all within a row
- gain_attn: bfloat16 [1024], P('dp'), may hold values from 0.5 to 1.5
- w_qkv: bfloat16 [3, 1024, 1024], P(None, 'dp', 'tensor'), may hold values from -0.1875 to 0.1875
- w_attn_out: bfloat16 [1024, 1024], P('tensor', 'dp'), may hold values from -0.5 to 0.5
- gain_mlp: bfloat16 [1024], P('dp'), may hold values from 0.5 to 1.5
- w_in: bfloat16 [2, 1024, 2624], P(None, 'dp', 'tensor'), may hold values from -0.1875 to 0.1875
- w_mlp_out: bfloat16 [2624, 1024], P('tensor', 'dp'), may hold values from -0.125 to 0.125
- cotangent: bfloat16 [4096, 1024], P(('dp', 'ctx')), may hold values from -6 to 6
Outputs:
- out_tokens: bfloat16 [4096, 1024], P(('dp', 'ctx'))
- grad_tokens: float32 [4096, 1024], P(('dp', 'ctx'))
- grad_gain_attn: float32 [1024], P('dp')
- grad_w_qkv: float32 [3, 1024, 1024], P(None, 'dp', 'tensor')
- grad_w_attn_out: float32 [1024, 1024], P('tensor', 'dp')
- grad_gain_mlp: float32 [1024], P('dp')
- grad_w_in: float32 [2, 1024, 2624], P(None, 'dp', 'tensor')
- grad_w_mlp_out: float32 [2624, 1024], P('tensor', 'dp')
Inputs may be any that keep to these rules, and one draw needn't show every extreme that they name: `doc_lengths`: each row sums to 1024, and the longest document of each row has exactly half of 1024 tokens.
All inputs are finite; a program needn't handle non-finite values.
Results may differ from a plain program's by a relative error of at most 0.013.
Values may be sent and summed in bfloat16 or wider, within the bound.
A program may use at most 128 MiB of HBM per device.

v0:
```python
import math

import jax
import jax.numpy as jnp
from jax import lax
from jax.sharding import PartitionSpec as P

HD = 64


NORM_EPS = 1e-05
ROPE_BASE = 160000.0
MASK_FILL = -1e30
INV_ROOT_TWO = 1.0 / math.sqrt(2.0)
INV_ROOT_TWO_PI = 1.0 / math.sqrt(2.0 * math.pi)


def norm_forward(x_float, gain_vec):
    row_mean = jnp.mean(x_float, axis=-1, keepdims=True)
    centered = x_float - row_mean
    inv_std = lax.rsqrt(jnp.mean(centered * centered, axis=-1, keepdims=True) + NORM_EPS)
    x_hat = centered * inv_std
    normed = (x_hat * gain_vec.astype(jnp.float32)).astype(jnp.bfloat16)
    return (x_hat, inv_std, normed)


def norm_backward(grad_out, x_hat, inv_std, gain_vec):
    grad_hat = grad_out * gain_vec.astype(jnp.float32)
    grad_gain = jnp.sum(grad_out * x_hat, axis=0)
    inner_term = (
        grad_hat
        - jnp.mean(grad_hat, axis=-1, keepdims=True)
        - x_hat * jnp.mean(grad_hat * x_hat, axis=-1, keepdims=True)
    )
    return (inv_std * inner_term, grad_gain)


def rope_tables(doc_len, span_len, head_width):
    doc_end = jnp.cumsum(doc_len)
    doc_start = doc_end - doc_len
    places = jnp.arange(span_len, dtype=jnp.int32)
    inside = places[:, None] >= doc_start[None, :]
    begins = jnp.max(jnp.where(inside, doc_start[None, :], 0), axis=1)
    segment = jnp.sum((places[:, None] >= doc_end[None, :]).astype(jnp.int32), axis=1)
    offset = (places - begins).astype(jnp.float32)
    half_width = head_width // 2
    frequency = ROPE_BASE ** (-(jnp.arange(half_width, dtype=jnp.float32) * (2.0 / head_width)))
    angles = offset[:, None] * frequency[None, :]
    angles = jnp.concatenate([angles, angles], axis=1)
    return (jnp.cos(angles), jnp.sin(angles), segment)


def rotate(values_in, cosines, sines):
    half_width = values_in.shape[-1] // 2
    turned = jnp.concatenate([-values_in[..., half_width:], values_in[..., :half_width]], axis=-1)
    return values_in * cosines[:, None, :] + turned * sines[:, None, :]


def rotate_back(grads_in, cosines, sines):
    half_width = grads_in.shape[-1] // 2
    scaled = grads_in * sines[:, None, :]
    turned = jnp.concatenate([scaled[..., half_width:], -scaled[..., :half_width]], axis=-1)
    return grads_in * cosines[:, None, :] + turned


def masked_scores(query_blk, keys_all, same_doc):
    score_scale = query_blk.shape[-1] ** (-0.5)
    scores = (
        jnp.einsum("bhe,che->hbc", query_blk, keys_all, preferred_element_type=jnp.float32)
        * score_scale
    )
    return jnp.where(same_doc[None, :, :], scores, MASK_FILL)


def attend_rows(query_blk, keys_all, vals_all, same_doc):
    scores = masked_scores(query_blk, keys_all, same_doc)
    row_max = jnp.max(scores, axis=-1, keepdims=True)
    expo_vals = jnp.exp(scores - row_max)
    row_total = jnp.sum(expo_vals, axis=-1, keepdims=True)
    prob_b = (expo_vals / row_total).astype(jnp.bfloat16)
    out_rows = jnp.einsum("hbc,che->bhe", prob_b, vals_all, preferred_element_type=jnp.float32)
    log_total = (row_max + jnp.log(row_total))[:, :, 0]
    return (out_rows.astype(jnp.bfloat16), log_total)


def attend_rows_back(query_blk, out_blk, grad_blk, log_blk, keys_all, vals_all, same_doc):
    score_scale = query_blk.shape[-1] ** (-0.5)
    scores = masked_scores(query_blk, keys_all, same_doc)
    probs = jnp.exp(scores - log_blk[:, :, None])
    prob_b = probs.astype(jnp.bfloat16)
    grad_vals = jnp.einsum("hbc,bhe->che", prob_b, grad_blk, preferred_element_type=jnp.float32)
    grad_prob = jnp.einsum("bhe,che->hbc", grad_blk, vals_all, preferred_element_type=jnp.float32)
    delta_row = jnp.sum(grad_blk.astype(jnp.float32) * out_blk.astype(jnp.float32), axis=-1).T
    grad_score = (probs * (grad_prob - delta_row[:, :, None]) * score_scale).astype(jnp.bfloat16)
    grad_query = jnp.einsum(
        "hbc,che->bhe", grad_score, keys_all, preferred_element_type=jnp.float32
    )
    grad_keys = jnp.einsum(
        "hbc,bhe->che", grad_score, query_blk, preferred_element_type=jnp.float32
    )
    return (grad_query, grad_keys, grad_vals)


def attention_forward(query_rot, keys_all, vals_all, segment):
    row_count, head_count, head_width = query_rot.shape
    block_rows = min(512, row_count)
    block_count = row_count // block_rows
    query_blocks = query_rot.reshape(block_count, block_rows, head_count, head_width)
    seg_blocks = segment.reshape(block_count, block_rows)

    def one_block(block_args):
        query_blk, seg_blk = block_args
        same_doc = seg_blk[:, None] == segment[None, :]
        return attend_rows(query_blk, keys_all, vals_all, same_doc)

    out_blocks, log_blocks = lax.map(one_block, (query_blocks, seg_blocks))
    return (out_blocks.reshape(row_count, head_count, head_width), log_blocks)


def attention_backward(query_rot, keys_all, vals_all, attn_heads, grad_heads, log_blocks, segment):
    row_count, head_count, head_width = query_rot.shape
    block_rows = min(512, row_count)
    block_count = row_count // block_rows
    shaped = (block_count, block_rows, head_count, head_width)

    def one_block(carry, block_args):
        keys_acc, vals_acc = carry
        query_blk, out_blk, grad_blk, log_blk, seg_blk = block_args
        same_doc = seg_blk[:, None] == segment[None, :]
        grad_query, grad_keys, grad_vals = attend_rows_back(
            query_blk, out_blk, grad_blk, log_blk, keys_all, vals_all, same_doc
        )
        return ((keys_acc + grad_keys, vals_acc + grad_vals), grad_query)

    zeros_acc = jnp.zeros((row_count, head_count, head_width), jnp.float32)
    (grad_keys, grad_vals), grad_query = lax.scan(
        one_block,
        (zeros_acc, zeros_acc),
        (
            query_rot.reshape(shaped),
            attn_heads.reshape(shaped),
            grad_heads.reshape(shaped),
            log_blocks,
            segment.reshape(block_count, block_rows),
        ),
    )
    return (grad_query.reshape(row_count, head_count, head_width), grad_keys, grad_vals)


def local(tokens, doc_lengths, gain_attn, w_qkv, w_attn_out, gain_mlp, w_in, w_mlp_out, cotangent):
    f32 = jnp.float32
    bf16 = jnp.bfloat16
    gathered = (
        lax.all_gather(gain_attn, "dp", axis=0, tiled=True),
        lax.all_gather(w_qkv, "dp", axis=1, tiled=True),
        lax.all_gather(w_attn_out, "dp", axis=1, tiled=True),
        lax.all_gather(gain_mlp, "dp", axis=0, tiled=True),
        lax.all_gather(w_in, "dp", axis=1, tiled=True),
        lax.all_gather(w_mlp_out, "dp", axis=1, tiled=True),
    )
    gain_one, w_query_all, w_out_all, gain_two, w_in_all, w_down_all = gathered
    ctx_ways = lax.axis_size("ctx")
    tok_rows = tokens.shape[0]
    span_len = tok_rows * ctx_ways
    local_width = w_query_all.shape[2]
    per_group = local_width // ctx_ways
    heads_here = per_group // HD
    cosines, sines, segment = rope_tables(doc_lengths[0], span_len, HD)
    x_float = tokens.astype(f32)
    hat_one, inv_one, normed_one = norm_forward(x_float, gain_one)
    projected = jnp.einsum(
        "td,kde->kte", normed_one, w_query_all, preferred_element_type=f32
    ).astype(bf16)
    projected = projected.reshape(3, tok_rows, ctx_ways, per_group)
    spread = lax.all_to_all(projected, "ctx", split_axis=2, concat_axis=1, tiled=True)
    spread = spread.reshape(3, span_len, heads_here, HD)
    query_rot = rotate(spread[0].astype(f32), cosines, sines).astype(bf16)
    keys_all = rotate(spread[1].astype(f32), cosines, sines).astype(bf16)
    vals_all = spread[2]
    attn_heads, log_blocks = attention_forward(query_rot, keys_all, vals_all, segment)
    returned = lax.all_to_all(
        attn_heads.reshape(span_len, 1, per_group), "ctx", split_axis=0, concat_axis=1, tiled=True
    )
    attn_flat = returned.reshape(tok_rows, local_width)
    attn_total = lax.psum(jnp.dot(attn_flat, w_out_all, preferred_element_type=f32), "tensor")
    mixed_one = x_float + attn_total
    hat_two, inv_two, normed_two = norm_forward(mixed_one, gain_two)
    pair_in = jnp.einsum("td,kde->kte", normed_two, w_in_all, preferred_element_type=f32)
    act_in = pair_in[0]
    gate_in = pair_in[1]
    cdf_val = 0.5 * (1.0 + jax.scipy.special.erf(act_in * INV_ROOT_TWO))
    gelu_val = act_in * cdf_val
    hidden = (gelu_val * gate_in).astype(bf16)
    mlp_total = lax.psum(jnp.dot(hidden, w_down_all, preferred_element_type=f32), "tensor")
    result = (mixed_one + mlp_total).astype(bf16)
    cot_float = cotangent.astype(f32)
    grad_mlp_out = jnp.einsum("tf,td->fd", hidden, cotangent, preferred_element_type=f32)
    grad_hidden = jnp.einsum("td,fd->tf", cotangent, w_down_all, preferred_element_type=f32)
    gelu_slope = cdf_val + act_in * jnp.exp(-0.5 * act_in * act_in) * INV_ROOT_TWO_PI
    grad_pair = jnp.stack(
        [(grad_hidden * gate_in * gelu_slope).astype(bf16), (grad_hidden * gelu_val).astype(bf16)]
    )
    grad_in = jnp.einsum("td,kte->kde", normed_two, grad_pair, preferred_element_type=f32)
    grad_normed_two = lax.psum(
        jnp.einsum("kte,kde->td", grad_pair, w_in_all, preferred_element_type=f32), "tensor"
    )
    back_two, grad_gain_mlp = norm_backward(grad_normed_two, hat_two, inv_two, gain_two)
    grad_mixed = cot_float + back_two
    grad_mixed_b = grad_mixed.astype(bf16)
    grad_attn_out = jnp.einsum("te,td->ed", attn_flat, grad_mixed_b, preferred_element_type=f32)
    grad_local = jnp.einsum(
        "td,ed->te", grad_mixed_b, w_out_all, preferred_element_type=f32
    ).astype(bf16)
    grad_spread = lax.all_to_all(
        grad_local.reshape(tok_rows, ctx_ways, per_group),
        "ctx",
        split_axis=1,
        concat_axis=0,
        tiled=True,
    )
    grad_heads = grad_spread.reshape(span_len, heads_here, HD)
    grad_query, grad_keys, grad_vals = attention_backward(
        query_rot, keys_all, vals_all, attn_heads, grad_heads, log_blocks, segment
    )
    grad_query = rotate_back(grad_query, cosines, sines).astype(bf16)
    grad_keys = rotate_back(grad_keys, cosines, sines).astype(bf16)
    grad_stack = jnp.stack([grad_query, grad_keys, grad_vals.astype(bf16)]).reshape(
        3, span_len, 1, per_group
    )
    grad_back = lax.all_to_all(grad_stack, "ctx", split_axis=1, concat_axis=2, tiled=True)
    grad_proj = grad_back.reshape(3, tok_rows, local_width)
    grad_qkv = jnp.einsum("td,kte->kde", normed_one, grad_proj, preferred_element_type=f32)
    grad_normed_one = lax.psum(
        jnp.einsum("kte,kde->td", grad_proj, w_query_all, preferred_element_type=f32), "tensor"
    )
    back_one, grad_gain_attn = norm_backward(grad_normed_one, hat_one, inv_one, gain_one)
    grad_tok = grad_mixed + back_one
    grad_parts = (grad_gain_attn, grad_qkv, grad_attn_out, grad_gain_mlp, grad_in, grad_mlp_out)
    owned = (
        lax.psum_scatter(grad_parts[0], "dp", scatter_dimension=0, tiled=True),
        lax.psum_scatter(grad_parts[1], "dp", scatter_dimension=1, tiled=True),
        lax.psum_scatter(grad_parts[2], "dp", scatter_dimension=1, tiled=True),
        lax.psum_scatter(grad_parts[3], "dp", scatter_dimension=0, tiled=True),
        lax.psum_scatter(grad_parts[4], "dp", scatter_dimension=1, tiled=True),
        lax.psum_scatter(grad_parts[5], "dp", scatter_dimension=1, tiled=True),
    )
    shares = (
        lax.psum_scatter(owned[0], "ctx", scatter_dimension=0, tiled=True),
        lax.psum_scatter(owned[1], "ctx", scatter_dimension=1, tiled=True),
        lax.psum_scatter(owned[2], "ctx", scatter_dimension=1, tiled=True),
        lax.psum_scatter(owned[3], "ctx", scatter_dimension=0, tiled=True),
        lax.psum_scatter(owned[4], "ctx", scatter_dimension=1, tiled=True),
        lax.psum_scatter(owned[5], "ctx", scatter_dimension=1, tiled=True),
    )
    owned = (
        lax.all_gather(shares[0], "ctx", axis=0, tiled=True),
        lax.all_gather(shares[1], "ctx", axis=1, tiled=True),
        lax.all_gather(shares[2], "ctx", axis=1, tiled=True),
        lax.all_gather(shares[3], "ctx", axis=0, tiled=True),
        lax.all_gather(shares[4], "ctx", axis=1, tiled=True),
        lax.all_gather(shares[5], "ctx", axis=1, tiled=True),
    )
    return (result, grad_tok, owned[0], owned[1], owned[2], owned[3], owned[4], owned[5])


def solution(mesh):
    in_specs = (
        P(("dp", "ctx"), None),
        P("dp", None),
        P("dp"),
        P(None, "dp", "tensor"),
        P("tensor", "dp"),
        P("dp"),
        P(None, "dp", "tensor"),
        P("tensor", "dp"),
        P(("dp", "ctx"), None),
    )
    out_specs = (
        P(("dp", "ctx"), None),
        P(("dp", "ctx"), None),
        P("dp"),
        P(None, "dp", "tensor"),
        P("tensor", "dp"),
        P("dp"),
        P(None, "dp", "tensor"),
        P("tensor", "dp"),
    )
    return jax.shard_map(local, mesh=mesh, in_specs=in_specs, out_specs=out_specs, check_vma=False)
```

profile of v0, /device:TPU:0, one launch (start us, length us, event | category | flops | bytes accessed | tf_op | source)
XLA Modules:
  0.0 1105.9 jit_solution(17320600677028368604)
XLA Ops:
  9.3 12.6 %all-gather = bf16[4,1,256]{2,1,0:T(2,128)(2,1)S(1)} all-gather(bf16[1,1,256]{2,1,0:T(2,128)(2,1)S(1)} %reshape.344), channel_id=1, replica_groups=mesh['dp'=4,'ctx'=4,'tensor'=2] {'dp'}, dimensions={0}, use_global_device_ids=true | all-gather | bytes 2560 | tf_op jit(solution)/shard_map/all_gather | solution.py:154
  26.3 4.4 fusion.79
  30.6 45.1 %all-gather.10.cloned.1.call-done = bf16[3,1024,512]{2,1,0:T(8,128)(2,1)} async-done(((bf16[3,256,512]{2,1,0:T(8,128)(2,1)}), bf16[3,1024,512]{2,1,0:T(8,128)(2,1)}) %all-gather.10.cloned.1.call-update) | async-done | bytes 3145744 | tf_op jit(solution)/shard_map/all_gather | solution.py:155
  75.8 3.0 fusion.45
  80.2 3.6 all-to-all-start
  85.6 9.1 all-to-all-done
  102.1 11.4 %while.27 = (s32[]{:T(128)}, bf16[2,512,2,64]{1,3,2,0:T(8,128)(2,1)}, f32[2,2,512]{2,1,0:T(2,128)S(1)}, s32[2,512]{1,0:T(2,128)S(1)}, s32[1024]{0:T(1024)S(1)}, ...) while((s32[]{:T(128)}, ...), condition=%wide.region_8.9_spmd, body=%wide.region_5.8_spmd.sunk | while | flops 281607168 | bytes 15509621 | solution.py:116
  102.5 2.0 fusion.136
  105.7 2.1 fusion.138
  108.2 2.0 fusion.136
  111.3 2.1 fusion.138
  115.7 2.2 reduce
  118.0 8.3 all_to_all.60
  126.8 2.7 fusion.89
  130.8 8.8 all-gather.1
  139.6 6.7 all-reduce.18.cloned.1.call-done
  148.0 100.8 %all-gather.14.cloned.1.call-done = bf16[2,1024,1312]{1,2,0:T(8,128)(2,1)} async-done(((bf16[2,256,1312]{1,2,0:T(8,128)(2,1)}), bf16[2,1024,1312]{1,2,0:T(8,128)(2,1)}) %all-gather.14.cloned.1.call-update) | async-done | bytes 5373968 | tf_op jit(solution)/shard_map/all_gather | solution.py:158
  248.8 5.8 convolution_bitcast_fusion.3
  254.6 49.7 %all-gather.16.cloned.1.call-done = bf16[1312,1024]{1,0:T(8,128)(2,1)} async-done(((bf16[1312,256]{1,0:T(8,128)(2,1)}), bf16[1312,1024]{1,0:T(8,128)(2,1)}) %all-gather.16.cloned.1.call-update) | async-done | bytes 2686992 | tf_op jit(solution)/shard_map/all_gather | solution.py:159
  304.3 4.0 fusion.61
  309.5 2.7 convolution_bitcast_fusion.6
  312.2 3.2 fusion.91
  315.5 14.4 %all-reduce.20.cloned.1.call-done = f32[256,1024]{1,0:T(8,128)} async-done(((f32[256,1024]{1,0:T(8,128)}), f32[256,1024]{1,0:T(8,128)}) %all-reduce.20.cloned.1.call-update) | async-done | bytes 1048592 | tf_op jit(solution)/shard_map/psum | solution.py:204
  329.9 2.3 multiply_reduce_fusion
  336.1 3.9 all-to-all-start.2
  340.3 5.6 all-to-all-done.2
  347.0 38.5 %while.28 = (s32[]{:T(128)}, f32[1024,2,64]{0,2,1:T(8,128)}, f32[1024,2,64]{0,2,1:T(8,128)}, f32[2,512,2,64]{1,0,3,2:T(2,128)}, bf16[2,512,2,64]{1,3,2,0:T(8,128...) while((s32[]{:T(128)}, f32[1024,2,64]{0,2,1:T(8,128)}, ...), condition=%wide.region_18.19_spmd.clone, body=%wide.region_16.18_spmd.clone.sunk | while | flops 683932672 | bytes 51677536 | solution.py:136
  350.4 2.9 multiply_convert_fusion.5
  353.4 2.3 fusion.151
  355.6 3.6 fusion.152
  360.3 5.8 dynamic_update_slice.20
  369.6 2.9 multiply_convert_fusion.5
  372.5 2.5 fusion.151
  374.9 3.7 fusion.152
  379.7 5.8 dynamic_update_slice.20
  391.7 15.9 %all_to_all.61 = bf16[3,1024,1,128]{3,0,2,1:T(4,128)(2,1)S(1)} all-to-all(bf16[3,1024,1,128]{3,0,2,1:T(4,128)(2,1)S(1)} %copy.130), channel_id=1, replica_groups=mesh['dp'=4,'ctx'=4,'tensor'=2] {'ctx'}, dimensions={1} | all-to-all | bytes 1572864 | tf_op jit(solution)/shard_map/all_to_all | solution.py:230
  408.7 3.7 convolution_bitcast_fusion.4
  413.8 5.8 convolution_bitcast_fusion.2
  420.8 1.8 fusion.73
  422.6 6.7 reduce-scatter.17.cloned.1.call-done
  429.3 2.9 copy.147
  432.3 110.7 %reduce-scatter.11.cloned.1.call-done = f32[3,256,512]{1,2,0:T(8,128)} async-done(((f32[3,1024,512]{1,2,0:T(8,128)}), f32[3,256,512]{1,2,0:T(8,128)}) %reduce-scatter.11.cloned.1.call-update) | async-done | bytes 1572880 | tf_op jit(solution)/shard_map/reduce_scatter | solution.py:241
  543.0 2.9 copy.134
  545.9 182.3 %reduce-scatter.15.cloned.1.call-done = f32[2,256,1312]{1,2,0:T(8,128)} async-done(((f32[2,1024,1312]{1,2,0:T(8,128)}), f32[2,256,1312]{1,2,0:T(8,128)}) %reduce-scatter.15.cloned.1.call-update) | async-done | bytes 2686992 | tf_op jit(solution)/shard_map/reduce_scatter | solution.py:244
  728.1 5.6 copy.137
  734.8 3.9 fusion.90
  738.7 2.0 convolution_bitcast_fusion.5
  740.7 34.2 %reduce-scatter.13.cloned.1.call-done = f32[512,256]{1,0:T(8,128)} async-done(((f32[512,1024]{1,0:T(8,128)}), f32[512,256]{1,0:T(8,128)}) %reduce-scatter.13.cloned.1.call-update) | async-done | bytes 524304 | tf_op jit(solution)/shard_map/reduce_scatter | solution.py:242
  775.0 2.0 copy.145
  777.1 31.0 %reduce-scatter.21.cloned.1.call-done = f32[64,1312]{1,0:T(8,128)} async-done(((f32[256,1312]{1,0:T(8,128)}), f32[64,1312]{1,0:T(8,128)}) %reduce-scatter.21.cloned.1.call-update) | async-done | bytes 335888
  809.5 119.2 %all-reduce.22.cloned.1.call-done = (f32[3,256,512]{2,0,1:T(4,128)}, f32[2,256,1312]{2,0,1:T(2,128)}) async-done(((f32[3,256,512]{2,0,1:T(4,128)}, f32[2,256,1312]{2,0,1:T(2,128)}), (f32[3,256,512]{2,0,1:T(4,128)}, f32[2,256,1312]{2,0,1:T(2,128)})) %all-reduce.22.cloned.1.call-update) | async-done | bytes 4259856
  930.8 2.1 constant_dynamic-slice_fusion.2
  934.8 18.3 %all-reduce.24.cloned.1.call-done = (f32[256,1024]{1,0:T(8,128)}, f32[256,1024]{1,0:T(8,128)}) async-done(((f32[256,1024]{1,0:T(8,128)}, f32[256,1024]{1,0:T(8,128)}), (f32[256,1024]{1,0:T(8,128)}, f32[256,1024]{1,0:T(8,128)})) %all-reduce.24.cloned.1.call-update) | async-done | bytes 2097168 | tf_op jit(solution)/shard_map/psum | solution.py:194
  953.1 1.7 fusion.58
  954.8 12.1 %all-reduce.11 = (f32[1024]{0:T(1024)S(1)}, f32[1024]{0:T(1024)S(1)}) all-reduce(f32[1024]{0:T(1024)S(1)} %get-tuple-element.309, f32[1024]{0:T(1024)S(1)} %copy-done.36), channel_id=2, replica_groups=mesh['dp'=4,'ctx'=4,'tensor'=2] {'dp'}, use_global_device_ids=true, to_apply=%region_23.24.clone | all-reduce | flops 2048 | bytes 16384
  967.1 9.8 all-reduce.9
  977.2 8.5 all-reduce.8
  985.7 2.2 add_convert_fusion
  989.3 11.2 %all_gather.44 = f32[512,256]{0,1:T(8,128)S(1)} all-gather(f32[512,64]{0,1:T(8,128)} %bitcast.247), channel_id=1, replica_groups=mesh['dp'=4,'ctx'=4,'tensor'=2] {'ctx'}, dimensions={1}, use_global_device_ids=true | all-gather | bytes 655360 | tf_op jit(solution)/shard_map/all_gather | solution.py:258
  1001.6 13.8 %all-gather.22.cloned.1.call-done = f32[1312,256]{0,1:T(8,128)} async-done(((f32[1312,64]{0,1:T(8,128)}), f32[1312,256]{0,1:T(8,128)}) %all-gather.22.cloned.1.call-update) | async-done | bytes 1343504 | tf_op jit(solution)/shard_map/all_gather | solution.py:261
  1015.3 2.8 copy.141
  1018.2 30.3 %all-gather.18.cloned.1.call-done = f32[3,256,512]{2,1,0:T(8,128)} async-done(((f32[3,64,512]{2,1,0:T(8,128)}), f32[3,256,512]{2,1,0:T(8,128)}) %all-gather.18.cloned.1.call-update) | async-done | bytes 1572880 | tf_op jit(solution)/shard_map/all_gather | solution.py:257
  1048.5 44.0 %all-gather.20.cloned.1.call-done = f32[2,256,1312]{2,0,1:T(2,128)} async-done(((f32[2,64,1312]{2,0,1:T(2,128)}), f32[2,256,1312]{2,0,1:T(2,128)}) %all-gather.20.cloned.1.call-update) | async-done | bytes 2686992 | tf_op jit(solution)/shard_map/all_gather | solution.py:260
  1092.4 5.5 copy.140
  (246 shorter events, 59.2 us)
Async XLA Ops:
  7.2 68.6 %copy-start.2 = (bf16[256,1024]{1,0:T(8,128)(2,1)S(1)}, bf16[256,1024]{1,0:T(8,128)(2,1)}, u32[]{:S(2)}) copy-start(bf16[256,1024]{1,0:T(8,128)(2,1)} %param.13) | copy-start | bytes 1572868
  7.2 68.6 %all-gather.10.cloned.1.call-start = ((), (), s32[]{:S(2)}) async-start(), calls=%async_computation.10 | async-start | bytes 3932160 | tf_op jit(solution)/shard_map/all_gather | solution.py:155
  7.9 118.9 %all-gather.12.cloned.1.call-start = ((), (), s32[]{:S(2)}) async-start(), calls=%async_computation.11 | async-start | bytes 1310720 | tf_op jit(solution)/shard_map/all_gather | solution.py:156
  22.0 386.7 %copy-start.32 = (f32[4,1,256]{2,1,0:T(1,128)}, f32[4,1,256]{2,1,0:T(1,128)S(1)}, u32[]{:S(2)}) copy-start(f32[4,1,256]{2,1,0:T(1,128)S(1)} %convert_element_type.155) | copy-start | bytes 12292
  23.2 385.5 %copy-start.34 = (f32[256]{0:T(256)}, f32[256]{0:T(256)S(1)}, u32[]{:S(2)}) copy-start(f32[256]{0:T(256)S(1)} %broadcast_multiply_fusion.9) | copy-start | bytes 3076
  24.5 384.1 %copy-start.37 = (f32[256]{0:T(256)}, f32[256]{0:T(256)S(1)}, u32[]{:S(2)}) copy-start(f32[256]{0:T(256)S(1)} %add_rsqrt_fusion.1) | copy-start | bytes 3076
  80.2 14.5 %all-to-all-start = ((bf16[3,256,4,128]{1,3,0,2:T(8,128)(2,1)}), bf16[3,256,4,128]{1,3,0,2:T(8,128)(2,1)S(1)}, u32[]{:S(2)}, u32[]{:S(2)}) async-start(bf16[3,256,4,128]{1,3,0,2:T(8,128)(2,1)} %copy.115), calls=%async_computation | async-start | bytes 1572864 | tf_op jit(solution)/shard_map/all_to_all | solution.py:175
  83.8 62.5 %all-reduce.18.cloned.1.call-start = ((), (), s32[]{:S(2)}) async-start(), calls=%async_computation.12 | async-start | bytes 2097152 | tf_op jit(solution)/shard_map/psum | solution.py:185
  85.6 16.4 %copy-start.10 = (f32[1024,64]{0,1:T(8,128)}, f32[1024,64]{0,1:T(8,128)S(1)}, u32[]{:S(2)}) copy-start(f32[1024,64]{0,1:T(8,128)S(1)} %get-tuple-element.383) | copy-start | bytes 786436
  85.6 16.4 %copy-start.15 = (f32[1024,64]{0,1:T(8,128)}, f32[1024,64]{0,1:T(8,128)S(1)}, u32[]{:S(2)}) copy-start(f32[1024,64]{0,1:T(8,128)S(1)} %get-tuple-element.384) | copy-start | bytes 786436
  98.7 2.8 copy-start.23
  113.5 13.3 %copy-start.30 = (bf16[1024,2,64]{0,2,1:T(8,128)(2,1)}, bf16[1024,2,64]{0,2,1:T(8,128)(2,1)S(1)}, u32[]{:S(2)}) copy-start(bf16[1024,2,64]{0,2,1:T(8,128)(2,1)S(1)} %get-tuple-element.680) | copy-start | bytes 786436
  126.6 4.2 copy-start.41
  126.8 12.9 %copy-start.17 = (bf16[256,4,1,128]{0,3,1,2:T(8,128)(2,1)}, bf16[256,4,1,128]{0,3,1,2:T(8,128)(2,1)S(1)}, u32[]{:S(2)}) copy-start(bf16[256,4,1,128]{0,3,1,2:T(8,128)(2,1)S(1)} %copy.123) | copy-start | bytes 786436
  129.6 119.2 %all-gather.14.cloned.1.call-start = ((), (), s32[]{:S(2)}) async-start(), calls=%async_computation.13 | async-start | bytes 6717440 | tf_op jit(solution)/shard_map/all_gather | solution.py:158
  130.1 174.2 %all-gather.16.cloned.1.call-start = ((), (), s32[]{:S(2)}) async-start(), calls=%async_computation.14 | async-start | bytes 3358720 | tf_op jit(solution)/shard_map/all_gather | solution.py:159
  130.7 199.2 %all-reduce.20.cloned.1.call-start = ((), (), s32[]{:S(2)}) async-start(), calls=%async_computation.15 | async-start | bytes 2097152 | tf_op jit(solution)/shard_map/psum | solution.py:204
  248.8 55.5 %copy-start.19 = (bf16[256,1024]{1,0:T(8,128)(2,1)S(1)}, bf16[256,1024]{1,0:T(8,128)(2,1)}, u32[]{:S(2)}) copy-start(bf16[256,1024]{1,0:T(8,128)(2,1)} %param.21) | copy-start | bytes 1572868
  304.3 5.1 copy-start.8
  308.4 1.1 copy-start.26
  308.4 3.8 copy-start.20
  312.1 117.2 %reduce-scatter.17.cloned.1.call-start = ((), (), s32[]{:S(2)}) async-start(), calls=%async_computation.21 | async-start | bytes 6717440 | tf_op jit(solution)/shard_map/reduce_scatter | solution.py:245
  315.4 19.3 %copy-start.12 = (bf16[512,1024]{1,0:T(8,128)(2,1)S(1)}, bf16[512,1024]{1,0:T(8,128)(2,1)}, u32[]{:S(2)}) copy-start(bf16[512,1024]{1,0:T(8,128)(2,1)} %all-gather.12.cloned.1.call-done) | copy-start | bytes 3145732
  333.8 1.0 copy-start.4
  336.1 9.7 all-to-all-start.2
  340.0 202.9 %reduce-scatter.11.cloned.1.call-start = ((), (), s32[]{:S(2)}) async-start(), calls=%async_computation.16 | async-start | bytes 7864320 | tf_op jit(solution)/shard_map/reduce_scatter | solution.py:241
  347.0 3.4 copy-start.31
  348.7 4.6 copy-start
  350.4 2.9 copy-start.6
  353.3 2.3 copy-start.7
  353.3 2.3 copy-start.28
  366.1 3.4 copy-start.31
  367.8 4.6 copy-start
  369.6 2.9 copy-start.6
  372.4 2.5 copy-start.7
  372.5 2.5 copy-start.28
  385.5 4.2 copy-start.1
  385.5 4.2 copy-start.16
  407.6 1.1 copy-start.3
  408.7 3.8 copy-start.13
  412.5 1.1 copy-start.25
  412.5 1.3 copy-start.27
  412.5 315.6 %reduce-scatter.15.cloned.1.call-start = ((), (), s32[]{:S(2)}) async-start(), calls=%async_computation.19 | async-start | bytes 13434880 | tf_op jit(solution)/shard_map/reduce_scatter | solution.py:244
  419.5 1.2 copy-start.5
  419.5 1.3 copy-start.18
  419.6 355.4 %reduce-scatter.13.cloned.1.call-start = ((), (), s32[]{:S(2)}) async-start(), calls=%async_computation.18 | async-start | bytes 2621440 | tf_op jit(solution)/shard_map/reduce_scatter | solution.py:242
  422.6 385.5 %reduce-scatter.21.cloned.1.call-start = ((), (), s32[]{:S(2)}) async-start(), calls=%async_computation.24 | async-start | bytes 1802240
  432.2 496.5 %all-reduce.22.cloned.1.call-start = ((), (), s32[]{:S(2)}) async-start(), calls=%async_computation.25 | async-start | bytes 9961472
  733.7 1.1 copy-start.21
  733.7 219.3 %all-reduce.24.cloned.1.call-start = ((), (), s32[]{:S(2)}) async-start(), calls=%async_computation.26 | async-start | bytes 4194304 | tf_op jit(solution)/shard_map/psum | solution.py:194
  734.8 3.9 copy-start.14
  734.8 3.9 copy-start.40
  740.7 67.5 %copy-start.39 = (u32[32]{0:T(128)S(1)}, u32[32]{0:T(128)}, u32[]{:S(2)}) copy-start(u32[32]{0:T(128)} %constant.85) | copy-start | bytes 388
  740.7 248.7 %reduce-scatter.19.cloned.1.call-start = ((), (), s32[]{:S(2)}) async-start(), calls=%async_computation.23 | async-start | bytes 655360
  777.0 155.8 %copy-start.42 = (u32[32]{0:T(128)S(1)}, u32[32]{0:T(128)}, u32[]{:S(2)}) copy-start(u32[32]{0:T(128)} %constant.97) | copy-start | bytes 388
  777.0 176.0 %copy-start.33 = (f32[4,1,256]{2,1,0:T(1,128)S(1)}, f32[4,1,256]{2,1,0:T(1,128)}, u32[]{:S(2)}) copy-start(f32[4,1,256]{2,1,0:T(1,128)} %copy-done.32) | copy-start | bytes 12292
  777.0 176.0 %copy-start.35 = (f32[256]{0:T(256)S(1)}, f32[256]{0:T(256)}, u32[]{:S(2)}) copy-start(f32[256]{0:T(256)} %copy-done.34) | copy-start | bytes 3076
  777.0 176.0 %copy-start.38 = (f32[256]{0:T(256)S(1)}, f32[256]{0:T(256)}, u32[]{:S(2)}) copy-start(f32[256]{0:T(256)} %copy-done.37) | copy-start | bytes 3076
  777.0 238.3 %all-gather.22.cloned.1.call-start = ((), (), s32[]{:S(2)}) async-start(), calls=%async_computation.22 | async-start | bytes 1802240 | tf_op jit(solution)/shard_map/all_gather | solution.py:261
  808.1 240.4 %all-gather.18.cloned.1.call-start = ((), (), s32[]{:S(2)}) async-start(), calls=%async_computation.17 | async-start | bytes 1966080 | tf_op jit(solution)/shard_map/all_gather | solution.py:257
  928.7 26.1 %copy-start.36 = (f32[1024]{0:T(1024)S(1)}, f32[1024]{0:T(1024)}, u32[]{:S(2)}) copy-start(f32[1024]{0:T(1024)} %get-tuple-element.307) | copy-start | bytes 12292
  930.7 161.7 %all-gather.20.cloned.1.call-start = ((), (), s32[]{:S(2)}) async-start(), calls=%async_computation.20 | async-start | bytes 3604480 | tf_op jit(solution)/shard_map/all_gather | solution.py:260
  985.7 2.3 copy-start.9
  1048.5 49.5 %copy-start.22 = (f32[3,256,512]{2,1,0:T(8,128)S(1)}, f32[3,256,512]{2,1,0:T(8,128)}, u32[]{:S(2)}) copy-start(f32[3,256,512]{2,1,0:T(8,128)} %all-gather.18.cloned.1.call-done) | copy-start | bytes 4718596
  (4 other events, 3.4 us)
Sparse Core Ops, SparseCore 0:
  9.6 66.1 all-gather.9
  77.4 28.5 all-gather.11
  129.7 16.6 all-reduce.17
  147.8 101.0 all-gather.13
  250.2 54.0 all-gather.15
  312.3 17.5 all-reduce.19
  332.2 97.0 reduce-scatter.16
  431.6 111.2 reduce-scatter.10
  545.3 182.7 reduce-scatter.14
  730.3 44.6 reduce-scatter.12
  778.5 29.5 reduce-scatter.20
  812.1 116.5 all-reduce.21
  931.6 21.3 all-reduce.23
  956.3 26.3 reduce-scatter.18
  984.4 30.9 all-gather.21
  1017.6 30.8 all-gather.17
  1050.7 41.6 all-gather.19
where the time goes:
time: 1110 us
  waiting for transfers between devices  825 us (74%)
  blocking collectives  87.3 us (8%)
  matrix products  70 us (6%)
  local copies, waits for them, and re-layouts  63.7 us (6%)
  other arithmetic  34 us (3%)
  between operations  16.9 us (2%)
    reduce_scatter x1, waiting for transfers between devices, local(): lax.psum_scatter(grad_parts[4], 'dp', scatter_dimension=1, tiled=True)  182 us
    unnamed x20, waiting for transfers between devices  153 us
    reduce_scatter x1, waiting for transfers between devices, local(): lax.psum_scatter(grad_parts[1], 'dp', scatter_dimension=1, tiled=True)  111 us
    all_gather x1, waiting for transfers between devices, local(): lax.all_gather(w_in, 'dp', axis=1, tiled=True)  101 us
    all_gather x1, waiting for transfers between devices, local(): lax.all_gather(w_mlp_out, 'dp', axis=1, tiled=True)  49.7 us
    all_gather x1, waiting for transfers between devices, local(): lax.all_gather(w_qkv, 'dp', axis=1, tiled=True)  45.1 us
    all_gather x1, waiting for transfers between devices, local(): lax.all_gather(shares[4], 'ctx', axis=1, tiled=True)  44 us
    reduce_scatter x1, waiting for transfers between devices, local(): lax.psum_scatter(grad_parts[2], 'dp', scatter_dimension=1, tiled=True)  34.2 us
  transfers between devices with their start and end apart: 19, of which 17 were waited for; matrix products, arithmetic and copies ran while one was open for 13% of the time, Pallas kernels for 0%

commit v1 on v0

v1 whole, which is shorter than its diff:
```python
import math

import jax
import jax.numpy as jnp
from jax import lax
from jax.sharding import PartitionSpec as P

HD = 64


NORM_EPS = 1e-05
ROPE_BASE = 160000.0
MASK_FILL = -1e30
INV_ROOT_TWO = 1.0 / math.sqrt(2.0)
INV_ROOT_TWO_PI = 1.0 / math.sqrt(2.0 * math.pi)


def norm_forward(x_float, gain_vec):
    row_mean = jnp.mean(x_float, axis=-1, keepdims=True)
    centered = x_float - row_mean
    inv_std = lax.rsqrt(jnp.mean(centered * centered, axis=-1, keepdims=True) + NORM_EPS)
    x_hat = centered * inv_std
    normed = (x_hat * gain_vec.astype(jnp.float32)).astype(jnp.bfloat16)
    return (x_hat, inv_std, normed)


def norm_backward(grad_out, x_hat, inv_std, gain_vec):
    grad_hat = grad_out * gain_vec.astype(jnp.float32)
    grad_gain = jnp.sum(grad_out * x_hat, axis=0)
    inner_term = (
        grad_hat
        - jnp.mean(grad_hat, axis=-1, keepdims=True)
        - x_hat * jnp.mean(grad_hat * x_hat, axis=-1, keepdims=True)
    )
    return (inv_std * inner_term, grad_gain)


def rope_tables(doc_len, span_len, head_width):
    doc_end = jnp.cumsum(doc_len)
    doc_start = doc_end - doc_len
    places = jnp.arange(span_len, dtype=jnp.int32)
    inside = places[:, None] >= doc_start[None, :]
    begins = jnp.max(jnp.where(inside, doc_start[None, :], 0), axis=1)
    segment = jnp.sum((places[:, None] >= doc_end[None, :]).astype(jnp.int32), axis=1)
    offset = (places - begins).astype(jnp.float32)
    half_width = head_width // 2
    frequency = ROPE_BASE ** (-(jnp.arange(half_width, dtype=jnp.float32) * (2.0 / head_width)))
    angles = offset[:, None] * frequency[None, :]
    angles = jnp.concatenate([angles, angles], axis=1)
    return (jnp.cos(angles), jnp.sin(angles), segment)


def rotate(values_in, cosines, sines):
    half_width = values_in.shape[-1] // 2
    turned = jnp.concatenate([-values_in[..., half_width:], values_in[..., :half_width]], axis=-1)
    return values_in * cosines[:, None, :] + turned * sines[:, None, :]


def rotate_back(grads_in, cosines, sines):
    half_width = grads_in.shape[-1] // 2
    scaled = grads_in * sines[:, None, :]
    turned = jnp.concatenate([scaled[..., half_width:], -scaled[..., :half_width]], axis=-1)
    return grads_in * cosines[:, None, :] + turned


def masked_scores(query_blk, keys_all, same_doc):
    score_scale = query_blk.shape[-1] ** (-0.5)
    scores = (
        jnp.einsum("bhe,che->hbc", query_blk, keys_all, preferred_element_type=jnp.float32)
        * score_scale
    )
    return jnp.where(same_doc[None, :, :], scores, MASK_FILL)


def attend_rows(query_blk, keys_all, vals_all, same_doc):
    scores = masked_scores(query_blk, keys_all, same_doc)
    row_max = jnp.max(scores, axis=-1, keepdims=True)
    expo_vals = jnp.exp(scores - row_max)
    row_total = jnp.sum(expo_vals, axis=-1, keepdims=True)
    prob_b = (expo_vals / row_total).astype(jnp.bfloat16)
    out_rows = jnp.einsum("hbc,che->bhe", prob_b, vals_all, preferred_element_type=jnp.float32)
    log_total = (row_max + jnp.log(row_total))[:, :, 0]
    return (out_rows.astype(jnp.bfloat16), log_total)


def attend_rows_back(query_blk, out_blk, grad_blk, log_blk, keys_all, vals_all, same_doc):
    score_scale = query_blk.shape[-1] ** (-0.5)
    scores = masked_scores(query_blk, keys_all, same_doc)
    probs = jnp.exp(scores - log_blk[:, :, None])
    prob_b = probs.astype(jnp.bfloat16)
    grad_vals = jnp.einsum("hbc,bhe->che", prob_b, grad_blk, preferred_element_type=jnp.float32)
    grad_prob = jnp.einsum("bhe,che->hbc", grad_blk, vals_all, preferred_element_type=jnp.float32)
    delta_row = jnp.sum(grad_blk.astype(jnp.float32) * out_blk.astype(jnp.float32), axis=-1).T
    grad_score = (probs * (grad_prob - delta_row[:, :, None]) * score_scale).astype(jnp.bfloat16)
    grad_query = jnp.einsum(
        "hbc,che->bhe", grad_score, keys_all, preferred_element_type=jnp.float32
    )
    grad_keys = jnp.einsum(
        "hbc,bhe->che", grad_score, query_blk, preferred_element_type=jnp.float32
    )
    return (grad_query, grad_keys, grad_vals)


BOTH = ("dp", "ctx")


def add_pair(part):
    part_b = part.astype(jnp.bfloat16)
    ways = lax.axis_size("tensor")
    total = part_b.astype(jnp.float32)
    for step in range(1, ways):
        pairs = [(src, (src + step) % ways) for src in range(ways)]
        total = total + lax.ppermute(part_b, "tensor", pairs).astype(jnp.float32)
    return total


def own_rows(block, axis):
    ways = lax.axis_size("ctx")
    rows = block.shape[axis] // ways
    return lax.dynamic_slice_in_dim(block, lax.axis_index("ctx") * rows, rows, axis)


def local(tokens, doc_lengths, gain_attn, w_qkv, w_attn_out, gain_mlp, w_in, w_mlp_out, cotangent):
    f32 = jnp.float32
    bf16 = jnp.bfloat16
    gains = lax.all_gather(jnp.stack([gain_attn, gain_mlp]), "dp", axis=1, tiled=True)
    gain_one, gain_two = gains[0], gains[1]
    w_query_all = lax.all_gather(own_rows(w_qkv, 1), BOTH, axis=1, tiled=True)
    w_out_all = lax.all_gather(own_rows(w_attn_out.T, 0), BOTH, axis=0, tiled=True)
    w_in_all = lax.all_gather(own_rows(w_in, 1), BOTH, axis=1, tiled=True)
    w_down_all = lax.all_gather(own_rows(w_mlp_out.T, 0), BOTH, axis=0, tiled=True)
    ctx_ways = lax.axis_size("ctx")
    tok_rows = tokens.shape[0]
    span_len = tok_rows * ctx_ways
    local_width = w_query_all.shape[2]
    per_group = local_width // ctx_ways
    heads_here = per_group // HD
    cosines, sines, segment = rope_tables(doc_lengths[0], span_len, HD)
    same_doc = segment[:, None] == segment[None, :]
    x_float = tokens.astype(f32)
    hat_one, inv_one, normed_one = norm_forward(x_float, gain_one)
    projected = jnp.einsum(
        "td,kde->kte", normed_one, w_query_all, preferred_element_type=f32
    ).astype(bf16)
    projected = projected.reshape(3, tok_rows, ctx_ways, per_group)
    spread = lax.all_to_all(projected, "ctx", split_axis=2, concat_axis=1, tiled=True)
    spread = spread.reshape(3, span_len, heads_here, HD)
    query_rot = rotate(spread[0].astype(f32), cosines, sines).astype(bf16)
    keys_all = rotate(spread[1].astype(f32), cosines, sines).astype(bf16)
    vals_all = spread[2]
    attn_heads, log_rows = attend_rows(query_rot, keys_all, vals_all, same_doc)
    returned = lax.all_to_all(
        attn_heads.reshape(span_len, 1, per_group), "ctx", split_axis=0, concat_axis=1, tiled=True
    )
    attn_flat = returned.reshape(tok_rows, local_width)
    attn_total = add_pair(
        jnp.einsum("te,de->td", attn_flat, w_out_all, preferred_element_type=f32)
    )
    mixed_one = x_float + attn_total
    hat_two, inv_two, normed_two = norm_forward(mixed_one, gain_two)
    pair_in = jnp.einsum("td,kde->kte", normed_two, w_in_all, preferred_element_type=f32)
    act_in = pair_in[0]
    gate_in = pair_in[1]
    cdf_val = 0.5 * (1.0 + jax.scipy.special.erf(act_in * INV_ROOT_TWO))
    gelu_val = act_in * cdf_val
    hidden = (gelu_val * gate_in).astype(bf16)
    mlp_total = add_pair(
        jnp.einsum("tf,df->td", hidden, w_down_all, preferred_element_type=f32)
    )
    result = (mixed_one + mlp_total).astype(bf16)
    cot_float = cotangent.astype(f32)
    grad_mlp_out = jnp.einsum("td,tf->df", cotangent, hidden, preferred_element_type=f32)
    share_down = lax.psum_scatter(
        grad_mlp_out.astype(bf16), BOTH, scatter_dimension=0, tiled=True
    )
    grad_hidden = jnp.einsum("td,df->tf", cotangent, w_down_all, preferred_element_type=f32)
    gelu_slope = cdf_val + act_in * jnp.exp(-0.5 * act_in * act_in) * INV_ROOT_TWO_PI
    grad_pair = jnp.stack(
        [(grad_hidden * gate_in * gelu_slope).astype(bf16), (grad_hidden * gelu_val).astype(bf16)]
    )
    grad_in = [
        jnp.einsum("td,te->de", normed_two, grad_pair[k], preferred_element_type=f32)
        for k in range(2)
    ]
    share_in = [
        lax.psum_scatter(grad_in[k].astype(bf16), BOTH, scatter_dimension=0, tiled=True)
        for k in range(2)
    ]
    grad_normed_two = add_pair(
        jnp.einsum("kte,kde->td", grad_pair, w_in_all, preferred_element_type=f32)
    )
    back_two, grad_gain_mlp = norm_backward(grad_normed_two, hat_two, inv_two, gain_two)
    grad_mixed = cot_float + back_two
    grad_mixed_b = grad_mixed.astype(bf16)
    grad_attn_out = jnp.einsum("td,te->de", grad_mixed_b, attn_flat, preferred_element_type=f32)
    share_out = lax.psum_scatter(
        grad_attn_out.astype(bf16), BOTH, scatter_dimension=0, tiled=True
    )
    grad_local = jnp.einsum(
        "td,de->te", grad_mixed_b, w_out_all, preferred_element_type=f32
    ).astype(bf16)
    grad_spread = lax.all_to_all(
        grad_local.reshape(tok_rows, ctx_ways, per_group),
        "ctx",
        split_axis=1,
        concat_axis=0,
        tiled=True,
    )
    grad_heads = grad_spread.reshape(span_len, heads_here, HD)
    grad_query, grad_keys, grad_vals = attend_rows_back(
        query_rot, attn_heads, grad_heads, log_rows, keys_all, vals_all, same_doc
    )
    grad_query = rotate_back(grad_query, cosines, sines).astype(bf16)
    grad_keys = rotate_back(grad_keys, cosines, sines).astype(bf16)
    grad_stack = jnp.stack([grad_query, grad_keys, grad_vals.astype(bf16)]).reshape(
        3, span_len, 1, per_group
    )
    grad_back = lax.all_to_all(grad_stack, "ctx", split_axis=1, concat_axis=2, tiled=True)
    grad_proj = grad_back.reshape(3, tok_rows, local_width)
    grad_qkv = [
        jnp.einsum("td,te->de", normed_one, grad_proj[k], preferred_element_type=f32)
        for k in range(3)
    ]
    share_qkv = lax.psum_scatter(
        jnp.concatenate(grad_qkv, axis=1).astype(bf16), BOTH, scatter_dimension=0, tiled=True
    )
    share_qkv = share_qkv.reshape(-1, 3, local_width).transpose(1, 0, 2)
    grad_normed_one = add_pair(
        jnp.einsum("kte,kde->td", grad_proj, w_query_all, preferred_element_type=f32)
    )
    back_one, grad_gain_attn = norm_backward(grad_normed_one, hat_one, inv_one, gain_one)
    grad_tok = grad_mixed + back_one
    gain_sums = lax.psum(jnp.stack([grad_gain_attn, grad_gain_mlp]), BOTH)
    gain_rows = gain_attn.shape[0]
    gain_own = lax.dynamic_slice_in_dim(
        gain_sums, lax.axis_index("dp") * gain_rows, gain_rows, 1
    )
    own_down = lax.all_gather(share_down, "ctx", axis=0, tiled=True).astype(f32).T
    own_in = lax.all_gather(jnp.stack(share_in), "ctx", axis=1, tiled=True).astype(f32)
    own_out = lax.all_gather(share_out, "ctx", axis=0, tiled=True).astype(f32).T
    own_qkv = lax.all_gather(share_qkv, "ctx", axis=1, tiled=True).astype(f32)
    return (result, grad_tok, gain_own[0], own_qkv, own_out, gain_own[1], own_in, own_down)


def solution(mesh):
    in_specs = (
        P(("dp", "ctx"), None),
        P("dp", None),
        P("dp"),
        P(None, "dp", "tensor"),
        P("tensor", "dp"),
        P("dp"),
        P(None, "dp", "tensor"),
        P("tensor", "dp"),
        P(("dp", "ctx"), None),
    )
    out_specs = (
        P(("dp", "ctx"), None),
        P(("dp", "ctx"), None),
        P("dp"),
        P(None, "dp", "tensor"),
        P("tensor", "dp"),
        P("dp"),
        P(None, "dp", "tensor"),
        P("tensor", "dp"),
    )
    return jax.shard_map(local, mesh=mesh, in_specs=in_specs, out_specs=out_specs, check_vma=False)
```

time: 1110 us -> 834 us (0.75)
  waiting for transfers between devices: 825 us -> 576 us
  local copies, waits for them, and re-layouts: 63.7 us -> 37.5 us
  blocking collectives: 87.3 us -> 107 us
  other arithmetic: 34 us -> 21.4 us
    reduce_scatter x4, waiting for transfers between devices: 334 us -> 182 us  [the longest x2 108 us: local(): lax.psum_scatter(grad_in[k].astype(bf16), BOTH, scatter_dimension=0, tile...]
    all_gather x7 -> x5, waiting for transfers between devices: 284 us -> 238 us  [the longest x1 86.8 us: local(): w_in_all = lax.all_gather(own_rows(w_in, 1), BOTH, axis=1, tiled=True)]
    psum x3 -> x0, waiting for transfers between devices: 39.4 us -> none  [the longest x1 18.3 us: local(): lax.psum(jnp.dot(hidden, w_down_all, preferred_element_type=f32), 'tensor')]
    psum x0 -> x1, blocking collectives: none -> 38.5 us  [local(): gain_sums = lax.psum(jnp.stack([grad_gain_attn, grad_gain_mlp]), BOTH)]
    unnamed x3 -> x0, blocking collectives: 30.4 us -> none
    unnamed x20 -> x11, waiting for transfers between devices: 153 us -> 134 us
    all_gather x3 -> x4, blocking collectives: 32.7 us -> 45.4 us  [the longest x1 12.7 us: local(): lax.all_gather(jnp.stack([gain_attn, gain_mlp]), 'dp', axis=1, tiled=True)]
    dynamic_update_slice x4 -> x0, local copies, waits for them, and re-layouts: 12.1 us -> none  [attention_backward(): lax.scan(one_block, (zeros_acc, zeros_acc), (query_rot.reshape(shaped), a...]
  transfers between devices with their start and end apart: 19 -> 16, of which waited for: 17 -> 16; matrix products, arithmetic and copies ran while one was open for 13% -> 13% of each run, Pallas kernels for 0% -> 0%
where the time goes in v1:
time: 834 us; the launch traced here: 826 us
  waiting for transfers between devices  576 us (69%)
  blocking collectives  107 us (13%)
  matrix products  59.8 us (7%)
  local copies, waits for them, and re-layouts  37.5 us (4%)
  other arithmetic  21.4 us (3%)
  between operations  15.3 us (2%)
  starting transfers between devices  8.54 us (1%)
    unnamed x11, waiting for transfers between devices  134 us
    reduce_scatter x2, waiting for transfers between devices, local(): lax.psum_scatter(grad_in[k].astype(bf16), BOTH, scatter_dimension=0, tile...  108 us
    all_gather x1, waiting for transfers between devices, local(): w_in_all = lax.all_gather(own_rows(w_in, 1), BOTH, axis=1, tiled=True)  86.8 us
    reduce_scatter x1, waiting for transfers between devices, local(): lax.psum_scatter(grad_mlp_out.astype(bf16), BOTH, scatter_dimension=0, ti...  72 us
    all_gather x1, waiting for transfers between devices, local(): lax.all_gather(own_rows(w_mlp_out.T, 0), BOTH, axis=0, tiled=True)  61.3 us
    all_gather x1, waiting for transfers between devices, local(): w_query_all = lax.all_gather(own_rows(w_qkv, 1), BOTH, axis=1, tiled=True)  55.1 us
    psum x1, blocking collectives, local(): gain_sums = lax.psum(jnp.stack([grad_gain_attn, grad_gain_mlp]), BOTH)  38.5 us
    unnamed x63, local copies, waits for them, and re-layouts  20.4 us
  transfers between devices with their start and end apart: 16, of which 16 were waited for; matrix products, arithmetic and copies ran while one was open for 13% of the time, Pallas kernels for 0%

profile of v1, /device:TPU:0, one launch (start us, length us, event | category | flops | bytes accessed | tf_op | source)
XLA Modules:
  0.0 825.8 jit_solution(13252264614928242169)
XLA Ops:
  7.3 1.8 constant_dynamic-slice_fusion.4
  9.1 1.0 constant_dynamic-slice_fusion.3
  11.2 1.0 copy.211
  14.1 12.7 %all_gather.28 = bf16[2,1024]{1,0:T(2,128)(2,1)S(1)} all-gather(bf16[2,256]{1,0:T(2,128)(2,1)S(1)} %pad_maximum_fusion.5), channel_id=1, replica_groups=mesh['dp'=4,'ctx'=4,'tensor'=2] {'dp'}, dimensions={1}, use_global_device_ids=true | all-gather | bytes 5120 | tf_op jit(solution)/shard_map/all_gather | solution.py:126
  26.9 55.1 %all-gather.6.cloned.1.call-done = bf16[3,1024,512]{2,1,0:T(8,128)(2,1)} async-done(((bf16[3,64,512]{2,1,0:T(8,128)(2,1)}), bf16[3,1024,512]{2,1,0:T(8,128)(2,1)}) %all-gather.6.cloned.1.call-update) | async-done | bytes 3145744 | tf_op jit(solution)/shard_map/all_gather | solution.py:128
  82.0 3.0 convolution_convert_fusion.7
  85.9 3.5 all-to-all-start
  91.2 7.9 all-to-all-done
  100.7 2.2 copy.172
  102.9 1.3 reshape.226
  105.7 2.9 fusion.2
  108.6 2.0 fusion
  110.7 2.8 fusion.27
  115.1 8.4 %all_to_all.60 = bf16[4,2,16384]{2,1,0:T(2,128)(2,1)S(1)} all-to-all(bf16[4,2,16384]{2,1,0:T(2,128)(2,1)S(1)} %reshape.237), channel_id=1, replica_groups=mesh['dp'=4,'ctx'=4,'tensor'=2] {'ctx'}, dimensions={0} | all-to-all | bytes 524288 | tf_op jit(solution)/shard_map/all_to_all | solution.py:152
  124.0 17.8 %all-gather.8.cloned.1.call-done = bf16[1024,512]{1,0:T(8,128)(2,1)} async-done(((bf16[64,512]{1,0:T(8,128)(2,1)}), bf16[1024,512]{1,0:T(8,128)(2,1)}) %all-gather.8.cloned.1.call-update) | async-done | bytes 1048592 | tf_op jit(solution)/shard_map/all_gather | solution.py:129
  141.8 1.7 convolution_convert_fusion.8
  143.6 1.9 collective-permute-done
  146.1 86.8 %all-gather.10.cloned.1.call-done = bf16[2,1024,1312]{2,1,0:T(8,128)(2,1)} async-done(((bf16[2,64,1312]{2,1,0:T(8,128)(2,1)}), bf16[2,1024,1312]{2,1,0:T(8,128)(2,1)}) %all-gather.10.cloned.1.call-update) | async-done | bytes 5373968 | tf_op jit(solution)/shard_map/all_gather | solution.py:130
  232.8 6.0 convolution_bitcast_fusion
  238.9 61.3 %all-gather.12.cloned.1.call-done = bf16[1024,1312]{1,0:T(8,128)(2,1)} async-done(((bf16[64,1312]{1,0:T(8,128)(2,1)}), bf16[1024,1312]{1,0:T(8,128)(2,1)}) %all-gather.12.cloned.1.call-update) | async-done | bytes 2686992 | tf_op jit(solution)/shard_map/all_gather | solution.py:131
  300.2 4.9 fusion.13
  305.9 2.7 convolution_convert_fusion.2
  308.7 3.9 convolution_convert_fusion.1
  312.6 5.0 fusion.17
  317.7 1.0 convolution_convert_fusion.9
  320.8 1.3 multiply_add_fusion
  323.1 1.5 convolution_convert_fusion.6
  324.9 2.1 fusion.7
  327.0 2.9 copy.207
  329.9 1.2 copy-done.3
  331.1 1.7 convolution_convert_fusion.10
  333.6 3.4 all-to-all-start.2
  337.1 9.5 %all-to-all-done.2 = bf16[256,4,128]{0,2,1:T(8,128)(2,1)S(1)} async-done(((bf16[256,4,128]{0,2,1:T(8,128)(2,1)}), bf16[256,4,128]{0,2,1:T(8,128)(2,1)S(1)}, u32[]{:S(2)}, u32[]{:S(2)}) %all-to-all-start.2) | async-done | bytes 262176 | tf_op jit(solution)/shard_map/all_to_all | solution.py:202
  347.1 6.6 fusion.28
  353.7 1.3 copy.188
  355.0 1.1 multiply_reduce_fusion.3
  356.1 6.8 multiply_convert_fusion
  362.9 1.4 convolution_bitcast_fusion.4
  365.6 1.1 copy.187
  366.7 1.1 copy.186
  367.8 23.5 %reduce-scatter.12.cloned.1.call-done = bf16[64,1312]{1,0:T(8,128)(2,1)} async-done(((bf16[1024,1312]{1,0:T(8,128)(2,1)}), bf16[64,1312]{1,0:T(8,128)(2,1)}) %reduce-scatter.12.cloned.1.call-update) | async-done | bytes 167952 | tf_op jit(solution)/shard_map/reduce_scatter | solution.py:186
  391.3 84.7 %reduce-scatter.14.cloned.1.call-done = bf16[64,1312]{1,0:T(8,128)(2,1)} async-done(((bf16[1024,1312]{1,0:T(8,128)(2,1)}), bf16[64,1312]{1,0:T(8,128)(2,1)}) %reduce-scatter.14.cloned.1.call-update) | async-done | bytes 167952 | tf_op jit(solution)/shard_map/reduce_scatter | solution.py:186
  476.0 1.8 pad_maximum_fusion.2
  478.1 3.0 pad_maximum_fusion.1
  481.1 14.9 %all_to_all.61 = bf16[3,1024,1,128]{3,0,2,1:T(4,128)(2,1)S(1)} all-to-all(bf16[3,1024,1,128]{3,0,2,1:T(4,128)(2,1)S(1)} %pad_maximum_fusion.1), channel_id=1, replica_groups=mesh['dp'=4,'ctx'=4,'tensor'=2] {'ctx'}, dimensions={1} | all-to-all | bytes 1572864 | tf_op jit(solution)/shard_map/all_to_all | solution.py:218
  498.4 1.9 pad_maximum_fusion
  500.3 4.7 copy.205
  505.6 1.2 reshape.223
  506.8 3.2 fusion.20
  510.0 1.9 collective-permute-done.3
  512.5 38.5 %psum.7 = f32[2,1024]{1,0:T(2,128)S(1)} all-reduce(f32[2,1024]{1,0:T(2,128)S(1)} %pad_maximum_fusion.4), channel_id=1, replica_groups=mesh['dp'=4,'ctx'=4,'tensor'=2] {'dp','ctx'}, use_global_device_ids=true, to_apply=%region_16.17 | all-reduce | flops 2048 | bytes 16384 | tf_op jit(solution)/shard_map/psum | solution.py:233
  551.7 1.4 fusion.36
  553.1 1.5 reduce-scatter.10.cloned.1.call-done
  554.6 9.5 %all_gather.33 = bf16[256,512]{1,0:T(8,128)(2,1)S(1)} all-gather(bf16[64,512]{1,0:T(8,128)(2,1)} %reduce-scatter.10.cloned.1.call-done), channel_id=1, replica_groups=mesh['dp'=4,'ctx'=4,'tensor'=2] {'ctx'}, dimensions={0}, use_global_device_ids=true | all-gather | bytes 327680 | tf_op jit(solution)/shard_map/all_gather | solution.py:240
  564.2 1.0 copy.196
  565.2 72.0 %reduce-scatter.18.cloned.1.call-done = bf16[64,1312]{1,0:T(8,128)(2,1)} async-done(((bf16[1024,1312]{1,0:T(8,128)(2,1)}), bf16[64,1312]{1,0:T(8,128)(2,1)}) %reduce-scatter.18.cloned.1.call-update) | async-done | bytes 167952 | tf_op jit(solution)/shard_map/reduce_scatter | solution.py:173
  637.1 11.2 %all_gather.35 = bf16[256,1312]{1,0:T(8,128)(2,1)S(1)} all-gather(bf16[64,1312]{1,0:T(8,128)(2,1)} %reduce-scatter.18.cloned.1.call-done), channel_id=1, replica_groups=mesh['dp'=4,'ctx'=4,'tensor'=2] {'ctx'}, dimensions={0}, use_global_device_ids=true | all-gather | bytes 839680 | tf_op jit(solution)/shard_map/all_gather | solution.py:238
  648.4 1.5 copy.198
  649.9 16.7 %all-gather.14.cloned.1.call-done = bf16[2,256,1312]{2,1,0:T(8,128)(2,1)} async-done(((bf16[2,64,1312]{2,1,0:T(8,128)(2,1)}), bf16[2,256,1312]{2,1,0:T(8,128)(2,1)}) %all-gather.14.cloned.1.call-update) | async-done | bytes 1343504 | tf_op jit(solution)/shard_map/all_gather | solution.py:239
  666.6 3.0 copy.197
  669.5 134.2 %reduce-scatter.16.cloned.1.call-done = bf16[64,1536]{1,0:T(8,128)(2,1)} async-done(((bf16[1024,1536]{1,0:T(8,128)(2,1)}), bf16[64,1536]{1,0:T(8,128)(2,1)}) %reduce-scatter.16.cloned.1.call-update) | async-done | bytes 196624
  803.7 1.1 copy.206
  805.1 12.0 %all_gather.32 = bf16[3,256,512]{2,1,0:T(8,128)(2,1)S(1)} all-gather(bf16[3,64,512]{2,1,0:T(8,128)(2,1)S(1)} %bitcast.158), channel_id=1, replica_groups=mesh['dp'=4,'ctx'=4,'tensor'=2] {'ctx'}, dimensions={1}, use_global_device_ids=true | all-gather | bytes 983040 | tf_op jit(solution)/shard_map/all_gather | solution.py:241
  817.1 1.4 convert_element_type.206
  (143 shorter events, 23.2 us)
Async XLA Ops:
  7.2 3.8 copy-start
  7.2 5.1 copy-start.20
  7.2 6.2 copy-start.22
  7.2 6.4 copy-start.23
  7.2 6.3 copy-start.24
  7.2 6.4 copy-start.4
  7.2 74.8 %all-gather.6.cloned.1.call-start = ((), (), s32[]{:S(2)}) async-start(), calls=%async_computation.9 | async-start | bytes 3342336 | tf_op jit(solution)/shard_map/all_gather | solution.py:128
  9.1 132.7 %all-gather.8.cloned.1.call-start = ((), (), s32[]{:S(2)}) async-start(), calls=%async_computation.10 | async-start | bytes 1114112 | tf_op jit(solution)/shard_map/all_gather | solution.py:129
  10.9 221.9 %all-gather.10.cloned.1.call-start = ((), (), s32[]{:S(2)}) async-start(), calls=%async_computation.11 | async-start | bytes 6127616 | tf_op jit(solution)/shard_map/all_gather | solution.py:130
  12.2 287.9 %all-gather.12.cloned.1.call-start = ((), (), s32[]{:S(2)}) async-start(), calls=%async_computation.12 | async-start | bytes 3063808 | tf_op jit(solution)/shard_map/all_gather | solution.py:131
  85.9 13.1 %all-to-all-start = ((bf16[3,256,4,128]{1,3,0,2:T(8,128)(2,1)}), bf16[3,256,4,128]{1,3,0,2:T(8,128)(2,1)S(1)}, u32[]{:S(2)}, u32[]{:S(2)}) async-start(bf16[3,256,4,128]{1,3,0,2:T(8,128)(2,1)} %copy.170), calls=%async_computation | async-start | bytes 1572864 | tf_op jit(solution)/shard_map/all_to_all | solution.py:146
  89.4 301.8 %reduce-scatter.12.cloned.1.call-start = ((), (), s32[]{:S(2)}) async-start(), calls=%async_computation.14 | async-start | bytes 3063808 | tf_op jit(solution)/shard_map/reduce_scatter | solution.py:186
  90.6 13.7 %copy-start.9 = (f32[1024,64]{0,1:T(8,128)}, f32[1024,64]{0,1:T(8,128)S(1)}, u32[]{:S(2)}) copy-start(f32[1024,64]{0,1:T(8,128)S(1)} %get-tuple-element.105) | copy-start | bytes 786436
  91.2 19.4 %copy-start.6 = (pred[1024,1024]{0,1:T(8,128)(4,1)}, pred[1024,1024]{0,1:T(8,128)(4,1)S(1)}, u32[]{:S(2)}) copy-start(pred[1024,1024]{0,1:T(8,128)(4,1)S(1)} %broadcast_compare_fusion) | copy-start | bytes 3145732
  104.2 1.1 copy-start.17
  105.3 3.3 copy-start.12
  105.7 5.0 copy-start.19
  108.6 4.8 copy-start.5
  113.5 10.0 %copy-start.15 = (bf16[2,64,1024]{2,1,0:T(8,128)(2,1)}, bf16[2,64,1024]{2,1,0:T(8,128)(2,1)S(1)}, u32[]{:S(2)}) copy-start(bf16[2,64,1024]{2,1,0:T(8,128)(2,1)S(1)} %fusion.27) | copy-start | bytes 786436
  143.6 2.0 collective-permute-start
  232.8 67.3 %copy-start.11 = (bf16[256,1024]{1,0:T(8,128)(2,1)S(1)}, bf16[256,1024]{1,0:T(8,128)(2,1)}, u32[]{:S(2)}) copy-start(bf16[256,1024]{1,0:T(8,128)(2,1)} %param.17) | copy-start | bytes 1572868
  305.0 0.8 copy-start.18
  305.0 12.7 %copy-start.8 = (bf16[256,1312]{0,1:T(8,128)(2,1)}, bf16[256,1312]{0,1:T(8,128)(2,1)S(1)}, u32[]{:S(2)}) copy-start(bf16[256,1312]{0,1:T(8,128)(2,1)S(1)} %get-tuple-element.82) | copy-start | bytes 2015236
  308.6 167.3 %reduce-scatter.14.cloned.1.call-start = ((), (), s32[]{:S(2)}) async-start(), calls=%async_computation.15 | async-start | bytes 3063808 | tf_op jit(solution)/shard_map/reduce_scatter | solution.py:186
  312.6 242.1 %reduce-scatter.10.cloned.1.call-start = ((), (), s32[]{:S(2)}) async-start(), calls=%async_computation.13 | async-start | bytes 1114112 | tf_op jit(solution)/shard_map/reduce_scatter | solution.py:196
  312.6 5.1 copy-start.21
  317.6 2.0 collective-permute-start.2
  318.8 2.1 collective-permute-start.1
  322.1 1.0 copy-start.2
  324.6 312.5 %reduce-scatter.18.cloned.1.call-start = ((), (), s32[]{:S(2)}) async-start(), calls=%async_computation.18 | async-start | bytes 3063808 | tf_op jit(solution)/shard_map/reduce_scatter | solution.py:173
  329.9 1.2 copy-start.3
  329.9 17.2 %copy-start.7 = (pred[1024,1024]{0,1:T(8,128)(4,1)S(1)}, pred[1024,1024]{0,1:T(8,128)(4,1)}, u32[]{:S(2)}) copy-start(pred[1024,1024]{0,1:T(8,128)(4,1)} %copy-done.6) | copy-start | bytes 3145732
  333.6 13.0 %all-to-all-start.2 = ((bf16[256,4,128]{0,2,1:T(8,128)(2,1)}), bf16[256,4,128]{0,2,1:T(8,128)(2,1)S(1)}, u32[]{:S(2)}, u32[]{:S(2)}) async-start(bf16[256,4,128]{0,2,1:T(8,128)(2,1)} %bitcast.26), calls=%async_computation.2 | async-start | bytes 524288 | tf_op jit(solution)/shard_map/all_to_all | solution.py:202
  337.1 329.5 %all-gather.14.cloned.1.call-start = ((), (), s32[]{:S(2)}) async-start(), calls=%async_computation.16 | async-start | bytes 1802240 | tf_op jit(solution)/shard_map/all_gather | solution.py:239
  347.1 6.7 copy-start.16
  356.1 6.8 copy-start.14
  362.9 1.4 copy-start.13
  364.3 1.0 copy-start.10
  477.8 326.0 %reduce-scatter.16.cloned.1.call-start = ((), (), s32[]{:S(2)}) async-start(), calls=%async_computation.17 | async-start | bytes 3342336
  509.9 2.0 collective-permute-start.3
  666.6 151.9 %copy-start.1 = (bf16[2,256,1312]{1,2,0:T(8,128)(2,1)S(1)}, bf16[2,256,1312]{1,2,0:T(8,128)(2,1)}, u32[]{:S(2)}) copy-start(bf16[2,256,1312]{1,2,0:T(8,128)(2,1)} %param.15) | copy-start | bytes 4030468
Sparse Core Ops, SparseCore 0:
  11.4 70.5 all-gather.5
  85.3 56.4 all-gather.7
  145.2 87.6 all-gather.9
  235.4 64.6 all-gather.11
  308.8 82.4 reduce-scatter.11
  393.4 82.5 reduce-scatter.13
  478.8 75.7 reduce-scatter.9
  556.9 80.1 reduce-scatter.17
  639.5 26.9 all-gather.13
  671.4 132.3 reduce-scatter.15

commit v2 on v1

--- a/solution.py
+++ b/solution.py
@@ -102,6 +102,7 @@
 
 
 BOTH = ("dp", "ctx")
+LANES = 128
 
 
 def add_pair(part):
@@ -123,25 +124,37 @@
 def local(tokens, doc_lengths, gain_attn, w_qkv, w_attn_out, gain_mlp, w_in, w_mlp_out, cotangent):
     f32 = jnp.float32
     bf16 = jnp.bfloat16
-    gains = lax.all_gather(jnp.stack([gain_attn, gain_mlp]), "dp", axis=1, tiled=True)
-    gain_one, gain_two = gains[0], gains[1]
-    w_query_all = lax.all_gather(own_rows(w_qkv, 1), BOTH, axis=1, tiled=True)
-    w_out_all = lax.all_gather(own_rows(w_attn_out.T, 0), BOTH, axis=0, tiled=True)
-    w_in_all = lax.all_gather(own_rows(w_in, 1), BOTH, axis=1, tiled=True)
-    w_down_all = lax.all_gather(own_rows(w_mlp_out.T, 0), BOTH, axis=0, tiled=True)
+    units = w_in.shape[2]
+    padded = -(-units // LANES) * LANES
+    local_width = w_qkv.shape[2]
+    gain_cols = jnp.pad(jnp.stack([gain_attn, gain_mlp], axis=1), ((0, 0), (0, LANES - 2)))
+    attn_block = own_rows(
+        jnp.concatenate([w_qkv[0], w_qkv[1], w_qkv[2], w_attn_out.T, gain_cols], axis=1), 0
+    )
+    attn_all = lax.all_gather(attn_block, BOTH, axis=0, tiled=True)
+    mlp_parts = jnp.stack([own_rows(w_in[0], 0), own_rows(w_in[1], 0), own_rows(w_mlp_out.T, 0)])
+    mlp_parts = jnp.pad(mlp_parts, ((0, 0), (0, 0), (0, padded - units)))
+    mlp_block = jnp.concatenate([mlp_parts[0], mlp_parts[1], mlp_parts[2]], axis=1)
+    mlp_block, attn_all = lax.optimization_barrier((mlp_block, attn_all))
+    mlp_all = lax.all_gather(mlp_block, BOTH, axis=0, tiled=True)
+    qkv_width = 3 * local_width
+    w_query_all = attn_all[:, :qkv_width]
+    w_out_all = attn_all[:, qkv_width : qkv_width + local_width]
+    gain_one = attn_all[:, qkv_width + local_width]
+    gain_two = attn_all[:, qkv_width + local_width + 1]
+    w_in_all = mlp_all[:, : 2 * padded]
+    w_down_all = mlp_all[:, 2 * padded :]
     ctx_ways = lax.axis_size("ctx")
     tok_rows = tokens.shape[0]
     span_len = tok_rows * ctx_ways
-    local_width = w_query_all.shape[2]
     per_group = local_width // ctx_ways
     heads_here = per_group // HD
     cosines, sines, segment = rope_tables(doc_lengths[0], span_len, HD)
     same_doc = segment[:, None] == segment[None, :]
     x_float = tokens.astype(f32)
     hat_one, inv_one, normed_one = norm_forward(x_float, gain_one)
-    projected = jnp.einsum(
-        "td,kde->kte", normed_one, w_query_all, preferred_element_type=f32
-    ).astype(bf16)
+    projected = jnp.dot(normed_one, w_query_all, preferred_element_type=f32).astype(bf16)
+    projected = jnp.stack(jnp.split(projected, 3, axis=1))
     projected = projected.reshape(3, tok_rows, ctx_ways, per_group)
     spread = lax.all_to_all(projected, "ctx", split_axis=2, concat_axis=1, tiled=True)
     spread = spread.reshape(3, span_len, heads_here, HD)
@@ -158,9 +171,9 @@
     )
     mixed_one = x_float + attn_total
     hat_two, inv_two, normed_two = norm_forward(mixed_one, gain_two)
-    pair_in = jnp.einsum("td,kde->kte", normed_two, w_in_all, preferred_element_type=f32)
-    act_in = pair_in[0]
-    gate_in = pair_in[1]
+    pair_in = jnp.dot(normed_two, w_in_all, preferred_element_type=f32)
+    act_in = pair_in[:, :padded]
+    gate_in = pair_in[:, padded:]
     cdf_val = 0.5 * (1.0 + jax.scipy.special.erf(act_in * INV_ROOT_TWO))
     gelu_val = act_in * cdf_val
     hidden = (gelu_val * gate_in).astype(bf16)
@@ -170,32 +183,26 @@
     result = (mixed_one + mlp_total).astype(bf16)
     cot_float = cotangent.astype(f32)
     grad_mlp_out = jnp.einsum("td,tf->df", cotangent, hidden, preferred_element_type=f32)
-    share_down = lax.psum_scatter(
-        grad_mlp_out.astype(bf16), BOTH, scatter_dimension=0, tiled=True
-    )
     grad_hidden = jnp.einsum("td,df->tf", cotangent, w_down_all, preferred_element_type=f32)
     gelu_slope = cdf_val + act_in * jnp.exp(-0.5 * act_in * act_in) * INV_ROOT_TWO_PI
-    grad_pair = jnp.stack(
-        [(grad_hidden * gate_in * gelu_slope).astype(bf16), (grad_hidden * gelu_val).astype(bf16)]
-    )
-    grad_in = [
-        jnp.einsum("td,te->de", normed_two, grad_pair[k], preferred_element_type=f32)
-        for k in range(2)
-    ]
-    share_in = [
-        lax.psum_scatter(grad_in[k].astype(bf16), BOTH, scatter_dimension=0, tiled=True)
-        for k in range(2)
-    ]
+    grad_pair = jnp.concatenate(
+        [(grad_hidden * gate_in * gelu_slope).astype(bf16), (grad_hidden * gelu_val).astype(bf16)],
+        axis=1,
+    )
+    grad_in = jnp.einsum("td,te->de", normed_two, grad_pair, preferred_element_type=f32)
+    share_mlp = lax.psum_scatter(
+        jnp.concatenate([grad_in.astype(bf16), grad_mlp_out.astype(bf16)], axis=1),
+        BOTH,
+        scatter_dimension=0,
+        tiled=True,
+    )
     grad_normed_two = add_pair(
-        jnp.einsum("kte,kde->td", grad_pair, w_in_all, preferred_element_type=f32)
+        jnp.einsum("te,de->td", grad_pair, w_in_all, preferred_element_type=f32)
     )
     back_two, grad_gain_mlp = norm_backward(grad_normed_two, hat_two, inv_two, gain_two)
     grad_mixed = cot_float + back_two
     grad_mixed_b = grad_mixed.astype(bf16)
     grad_attn_out = jnp.einsum("td,te->de", grad_mixed_b, attn_flat, preferred_element_type=f32)
-    share_out = lax.psum_scatter(
-        grad_attn_out.astype(bf16), BOTH, scatter_dimension=0, tiled=True
-    )
     grad_local = jnp.einsum(
         "td,de->te", grad_mixed_b, w_out_all, preferred_element_type=f32
     ).astype(bf16)
@@ -217,28 +224,31 @@
     )
     grad_back = lax.all_to_all(grad_stack, "ctx", split_axis=1, concat_axis=2, tiled=True)
     grad_proj = grad_back.reshape(3, tok_rows, local_width)
-    grad_qkv = [
-        jnp.einsum("td,te->de", normed_one, grad_proj[k], preferred_element_type=f32)
-        for k in range(3)
-    ]
-    share_qkv = lax.psum_scatter(
-        jnp.concatenate(grad_qkv, axis=1).astype(bf16), BOTH, scatter_dimension=0, tiled=True
-    )
-    share_qkv = share_qkv.reshape(-1, 3, local_width).transpose(1, 0, 2)
+    grad_proj = jnp.concatenate([grad_proj[0], grad_proj[1], grad_proj[2]], axis=1)
+    grad_qkv = jnp.einsum("td,te->de", normed_one, grad_proj, preferred_element_type=f32)
     grad_normed_one = add_pair(
-        jnp.einsum("kte,kde->td", grad_proj, w_query_all, preferred_element_type=f32)
+        jnp.einsum("te,de->td", grad_proj, w_query_all, preferred_element_type=f32)
     )
     back_one, grad_gain_attn = norm_backward(grad_normed_one, hat_one, inv_one, gain_one)
     grad_tok = grad_mixed + back_one
-    gain_sums = lax.psum(jnp.stack([grad_gain_attn, grad_gain_mlp]), BOTH)
-    gain_rows = gain_attn.shape[0]
-    gain_own = lax.dynamic_slice_in_dim(
-        gain_sums, lax.axis_index("dp") * gain_rows, gain_rows, 1
-    )
-    own_down = lax.all_gather(share_down, "ctx", axis=0, tiled=True).astype(f32).T
-    own_in = lax.all_gather(jnp.stack(share_in), "ctx", axis=1, tiled=True).astype(f32)
-    own_out = lax.all_gather(share_out, "ctx", axis=0, tiled=True).astype(f32).T
-    own_qkv = lax.all_gather(share_qkv, "ctx", axis=1, tiled=True).astype(f32)
+    gain_grads = jnp.pad(
+        jnp.stack([grad_gain_attn, grad_gain_mlp], axis=1), ((0, 0), (0, LANES - 2))
+    )
+    share_attn = lax.psum_scatter(
+        jnp.concatenate(
+            [grad_qkv.astype(bf16), grad_attn_out.astype(bf16), gain_grads.astype(bf16)], axis=1
+        ),
+        BOTH,
+        scatter_dimension=0,
+        tiled=True,
+    )
+    own_mlp = lax.all_gather(share_mlp, "ctx", axis=0, tiled=True)
+    own_attn = lax.all_gather(share_attn, "ctx", axis=0, tiled=True)
+    own_in = jnp.stack([own_mlp[:, :units], own_mlp[:, padded : padded + units]]).astype(f32)
+    own_down = own_mlp[:, 2 * padded : 2 * padded + units].astype(f32).T
+    own_qkv = jnp.stack(jnp.split(own_attn[:, :qkv_width], 3, axis=1)).astype(f32)
+    own_out = own_attn[:, qkv_width : qkv_width + local_width].astype(f32).T
+    gain_own = own_attn[:, qkv_width + local_width : qkv_width + local_width + 2].astype(f32).T
     return (result, grad_tok, gain_own[0], own_qkv, own_out, gain_own[1], own_in, own_down)
 
 

time: 834 us -> 667 us (0.80)
  blocking collectives: 107 us -> 11.1 us
  waiting for transfers between devices: 576 us -> 499 us
  other arithmetic: 21.4 us -> 37.9 us
  matrix products: 59.8 us -> 46.7 us
    unnamed x11 -> x6, waiting for transfers between devices: 134 us -> 0.1 us
    reduce_scatter x4 -> x2, waiting for transfers between devices: 182 us -> 261 us  [the longest x1 171 us: local(): lax.psum_scatter(jnp.concatenate([grad_in.astype(bf16), grad_mlp_out.asty...]
    all_gather x4 -> x0, blocking collectives: 45.4 us -> none  [the longest x1 12.7 us: local(): lax.all_gather(jnp.stack([gain_attn, gain_mlp]), 'dp', axis=1, tiled=True)]
    psum x1 -> x0, blocking collectives: 38.5 us -> none  [local(): gain_sums = lax.psum(jnp.stack([grad_gain_attn, grad_gain_mlp]), BOTH)]
    all_gather x5 -> x4, waiting for transfers between devices: 238 us -> 205 us  [the longest x1 78.4 us: local(): attn_all = lax.all_gather(attn_block, BOTH, axis=0, tiled=True)]
    all_to_all x1 -> x0, blocking collectives: 14.9 us -> none  [local(): lax.all_to_all(grad_stack, 'ctx', split_axis=1, concat_axis=2, tiled=True)]
    all_to_all x0 -> x1, waiting for transfers between devices: none -> 13.3 us  [local(): lax.all_to_all(grad_stack, 'ctx', split_axis=1, concat_axis=2, tiled=True)]
    dot_general x9 -> x6, matrix products: 25.5 us -> 16.9 us  [the longest x1 4.51 us: local(): pair_in = jnp.dot(normed_two, w_in_all, preferred_element_type=f32)]
  transfers between devices with their start and end apart: 16 -> 13, of which waited for: 16 -> 12; matrix products, arithmetic and copies ran while one was open for 13% -> 7% of each run, Pallas kernels for 0% -> 0%
where the time goes in v2:
time: 667 us; the launch traced here: 658 us
  waiting for transfers between devices  499 us (75%)
  matrix products  46.7 us (7%)
  other arithmetic  37.9 us (6%)
  local copies, waits for them, and re-layouts  34.6 us (5%)
  between operations  15.5 us (2%)
  starting transfers between devices  12.6 us (2%)
  blocking collectives  11.1 us (2%)
    reduce_scatter x1, waiting for transfers between devices, local(): lax.psum_scatter(jnp.concatenate([grad_in.astype(bf16), grad_mlp_out.asty...  171 us
    reduce_scatter x1, waiting for transfers between devices, local(): lax.psum_scatter(jnp.concatenate([grad_qkv.astype(bf16), grad_attn_out.as...  89.6 us
    all_gather x1, waiting for transfers between devices, local(): attn_all = lax.all_gather(attn_block, BOTH, axis=0, tiled=True)  78.4 us
    all_gather x1, waiting for transfers between devices, local(): mlp_all = lax.all_gather(mlp_block, BOTH, axis=0, tiled=True)  67.7 us
    all_gather x1, waiting for transfers between devices, local(): own_mlp = lax.all_gather(share_mlp, 'ctx', axis=0, tiled=True)  32.2 us
    all_gather x1, waiting for transfers between devices, local(): own_attn = lax.all_gather(share_attn, 'ctx', axis=0, tiled=True)  26.3 us
  transfers between devices with their start and end apart: 13, of which 12 were waited for; matrix products, arithmetic and copies ran while one was open for 7% of the time, Pallas kernels for 0%

profile of v2, /device:TPU:0, one launch (start us, length us, event | category | flops | bytes accessed | tf_op | source)
XLA Modules:
  0.0 657.7 jit_solution(7090944337605879477)
XLA Ops:
  8.9 1.1 copy.153
  10.0 1.0 bitcast_dynamic-update-slice_fusion.3
  10.9 1.0 bitcast_dynamic-update-slice_fusion.2
  11.9 1.0 bitcast_dynamic-update-slice_fusion.1
  15.8 78.4 %all-gather.5.cloned.1.call-done = bf16[1024,2176]{1,0:T(8,128)(2,1)} async-done(((bf16[64,2176]{1,0:T(8,128)(2,1)}), bf16[1024,2176]{1,0:T(8,128)(2,1)}) %all-gather.5.cloned.1.call-update) | async-done | bytes 4456464 | tf_op jit(solution)/shard_map/all_gather | solution.py:134
  95.1 1.3 convert_reduce_fusion.1
  96.5 3.0 fusion.18
  100.8 3.5 all-to-all-start
  104.4 1.0 fusion.74
  106.1 11.5 %all-to-all-done = bf16[3,256,4,128]{3,1,0,2:T(8,128)(2,1)S(1)} async-done(((bf16[3,256,4,128]{3,1,0,2:T(8,128)(2,1)}), bf16[3,256,4,128]{3,1,0,2:T(8,128)(2,1)S(1)}, u32[]{:S(2)}, u32[]{:S(2)}) %all-to-all-start) | async-done | bytes 786464 | tf_op jit(solution)/shard_map/all_to_all | solution.py:159
  117.6 1.1 slice_convert_fusion
  118.6 1.3 copy.160
  121.3 2.0 copy.159
  123.3 1.3 reshape.240
  125.0 1.9 fusion.8
  127.0 2.0 fusion.1
  129.0 1.2 copy-done.3
  130.2 2.8 fusion.45
  134.6 11.1 %all_to_all.60 = bf16[4,2,16384]{2,1,0:T(2,128)(2,1)S(1)} all-to-all(bf16[4,2,16384]{2,1,0:T(2,128)(2,1)S(1)} %reshape.247), channel_id=1, replica_groups=mesh['dp'=4,'ctx'=4,'tensor'=2] {'ctx'}, dimensions={0} | all-to-all | bytes 524288 | tf_op jit(solution)/shard_map/all_to_all | solution.py:165
  146.1 1.8 convolution_convert_fusion.4
  148.0 1.9 collective-permute-done
  150.4 67.7 %all-gather.7.cloned.1.call-done = bf16[1024,4224]{1,0:T(8,128)(2,1)} async-done(((bf16[64,4224]{1,0:T(8,128)(2,1)}), bf16[1024,4224]{1,0:T(8,128)(2,1)}) %all-gather.7.cloned.1.call-update) | async-done | bytes 8650768 | tf_op jit(solution)/shard_map/all_gather | solution.py:139
  218.2 4.5 fusion.5
  223.5 1.4 fusion.29
  224.9 1.7 fusion.36
  226.7 1.0 fusion.33
  229.8 1.3 multiply_add_fusion
  231.1 1.7 convolution_convert_fusion.5
  233.6 3.6 all-to-all-start.2
  237.3 6.0 all-to-all-done.2
  244.2 1.1 reshape.238
  245.4 6.9 %fusion.46 = bf16[2,64,1024]{2,1,0:T(8,128)(2,1)} fusion(bf16[1024,2,64]{0,2,1:T(8,128)(2,1)S(1)} %reshape.238, f32[2,1024,1024]{1,2,0:T(8,128)} %copy-done.3, f32[2,1024]{1,0:T(2,128)S(1)} %log_add_fusion, pred[1024,1024]{0,1:T(8,128)(4,1)} %copy-done.4), kind=kOutput, calls=%fused_computation.64 | convolution fusion | flops 276955136 | bytes 9969664 | tf_op jit(solution)/shard_map/hbc,bhe->che/dot_general | solution.py:91
  252.3 5.6 multiply_convert_fusion
  257.9 1.4 convolution_bitcast_fusion.1
  259.3 1.7 broadcast_multiply_fusion.1
  261.8 2.0 copy.173
  263.8 1.1 fusion.93
  264.8 2.2 fusion.71
  267.0 1.3 copy.172
  268.3 1.9 copy.171
  270.3 4.0 pad_maximum_fusion.2
  274.2 4.2 all-to-all-start.3
  278.8 13.3 %all-to-all-done.3 = bf16[3,1024,1,128]{3,0,2,1:T(4,128)(2,1)} async-done(((bf16[3,1024,1,128]{3,0,2,1:T(4,128)(2,1)}), bf16[3,1024,1,128]{3,0,2,1:T(4,128)(2,1)}, u32[]{:S(2)}, u32[]{:S(2)}) %all-to-all-start.3) | async-done | bytes 786464 | tf_op jit(solution)/shard_map/all_to_all | solution.py:225
  292.0 1.3 copy.174
  294.6 3.1 fusion.30
  297.8 1.5 convolution_convert_fusion.3
  299.3 2.9 convolution_convert_fusion.2
  303.2 3.9 fusion.7
  307.1 1.0 copy-done.7
  308.2 2.2 fusion.13
  310.4 1.8 convolution_convert_fusion
  312.2 3.7 pad_maximum_fusion
  316.1 89.6 %reduce-scatter.3.cloned.1.call-done = bf16[64,2176]{1,0:T(8,128)(2,1)} async-done(((bf16[1024,2176]{1,0:T(8,128)(2,1)}), bf16[64,2176]{1,0:T(8,128)(2,1)}) %reduce-scatter.3.cloned.1.call-update) | async-done | bytes 278544 | tf_op jit(solution)/shard_map/reduce_scatter | solution.py:237
  405.7 171.5 %reduce-scatter.5.cloned.1.call-done = bf16[64,4224]{1,0:T(8,128)(2,1)} async-done(((bf16[1024,4224]{1,0:T(8,128)(2,1)}), bf16[64,4224]{1,0:T(8,128)(2,1)}) %reduce-scatter.5.cloned.1.call-update) | async-done | bytes 540688 | tf_op jit(solution)/shard_map/reduce_scatter | solution.py:193
  577.3 1.4 fusion.56
  578.7 26.3 %all-gather.9.cloned.1.call-done = bf16[256,2176]{1,0:T(8,128)(2,1)} async-done(((bf16[64,2176]{1,0:T(8,128)(2,1)}), bf16[256,2176]{1,0:T(8,128)(2,1)}) %all-gather.9.cloned.1.call-update) | async-done | bytes 1114128 | tf_op jit(solution)/shard_map/all_gather | solution.py:246
  604.9 1.3 convert_bitcast_fusion.1
  606.3 1.0 copy.181
  608.9 1.3 maximum_convert_fusion.1
  610.2 32.2 %all-gather.11.cloned.1.call-done = bf16[256,4224]{1,0:T(8,128)(2,1)} async-done(((bf16[64,4224]{1,0:T(8,128)(2,1)}), bf16[256,4224]{1,0:T(8,128)(2,1)}) %all-gather.11.cloned.1.call-update) | async-done | bytes 2162704 | tf_op jit(solution)/shard_map/all_gather | solution.py:245
  642.4 2.8 convert_bitcast_fusion
  645.2 1.5 copy.183
  646.7 1.6 maximum_convert_fusion
  648.3 2.1 copy.182
  (159 shorter events, 21.8 us)
Async XLA Ops:
  7.2 6.6 %copy-start = (bf16[1312,256]{1,0:T(8,128)(2,1)S(1)}, bf16[1312,256]{1,0:T(8,128)(2,1)}, u32[]{:S(2)}) copy-start(bf16[1312,256]{1,0:T(8,128)(2,1)} %param.16) | copy-start | bytes 2015236
  7.2 6.9 %copy-start.14 = (bf16[2,256,1312]{1,2,0:T(8,128)(2,1)S(1)}, bf16[2,256,1312]{1,2,0:T(8,128)(2,1)}, u32[]{:S(2)}) copy-start(bf16[2,256,1312]{1,2,0:T(8,128)(2,1)} %param.15) | copy-start | bytes 4030468
  7.2 87.0 %all-gather.5.cloned.1.call-start = ((), (), s32[]{:S(2)}) async-start(), calls=%async_computation.6 | async-start | bytes 4734976 | tf_op jit(solution)/shard_map/all_gather | solution.py:134
  13.7 204.5 %all-gather.7.cloned.1.call-start = ((), (), s32[]{:S(2)}) async-start(), calls=%async_computation.7 | async-start | bytes 9191424 | tf_op jit(solution)/shard_map/all_gather | solution.py:139
  14.2 80.0 %copy-start.33 = (s32[1,8]{1,0:T(1,128)S(1)}, s32[1,8]{1,0:T(1,128)}, u32[]{:S(2)}) copy-start(s32[1,8]{1,0:T(1,128)} %param.10) | copy-start | bytes 100
  14.2 80.4 %copy-start.2 = (bf16[256,1024]{1,0:T(8,128)(2,1)S(1)}, bf16[256,1024]{1,0:T(8,128)(2,1)}, u32[]{:S(2)}) copy-start(bf16[256,1024]{1,0:T(8,128)(2,1)} %param.9) | copy-start | bytes 1572868
  94.8 4.6 copy-start.28
  95.1 4.4 copy-start.30
  100.8 16.7 %all-to-all-start = ((bf16[3,256,4,128]{3,1,0,2:T(8,128)(2,1)}), bf16[3,256,4,128]{3,1,0,2:T(8,128)(2,1)S(1)}, u32[]{:S(2)}, u32[]{:S(2)}) async-start(bf16[3,256,4,128]{3,1,0,2:T(8,128)(2,1)} %pad_maximum_fusion.5), calls=%async_computation | async-start | bytes 1572864 | tf_op jit(solution)/shard_map/all_to_all | solution.py:159
  105.4 19.3 %copy-start.8 = (f32[1024,64]{0,1:T(8,128)}, f32[1024,64]{0,1:T(8,128)S(1)}, u32[]{:S(2)}) copy-start(f32[1024,64]{0,1:T(8,128)S(1)} %get-tuple-element.112) | copy-start | bytes 786436
  106.1 22.9 %copy-start.4 = (pred[1024,1024]{0,1:T(8,128)(4,1)}, pred[1024,1024]{0,1:T(8,128)(4,1)S(1)}, u32[]{:S(2)}) copy-start(pred[1024,1024]{0,1:T(8,128)(4,1)S(1)} %broadcast_compare_fusion) | copy-start | bytes 3145732
  125.0 1.9 copy-start.15
  125.0 1.9 copy-start.17
  127.0 3.2 copy-start.3
  127.0 3.2 copy-start.25
  146.1 76.6 %copy-start.19 = (bf16[256,4,1,128]{0,3,1,2:T(8,128)(2,1)}, bf16[256,4,1,128]{0,3,1,2:T(8,128)(2,1)S(1)}, u32[]{:S(2)}) copy-start(bf16[256,4,1,128]{0,3,1,2:T(8,128)(2,1)S(1)} %copy.163) | copy-start | bytes 786436
  147.9 2.0 collective-permute-start
  218.2 4.5 copy-start.9
  218.2 5.3 copy-start.32
  224.9 1.7 copy-start.21
  224.9 1.7 copy-start.23
  224.9 1.8 copy-start.6
  226.7 2.0 collective-permute-start.2
  227.8 2.1 collective-permute-start.1
  233.6 9.6 %all-to-all-start.2 = ((bf16[256,4,128]{0,2,1:T(8,128)(2,1)}), bf16[256,4,128]{0,2,1:T(8,128)(2,1)S(1)}, u32[]{:S(2)}, u32[]{:S(2)}) async-start(bf16[256,4,128]{0,2,1:T(8,128)(2,1)} %bitcast.107), calls=%async_computation.2 | async-start | bytes 524288 | tf_op jit(solution)/shard_map/all_to_all | solution.py:209
  245.4 6.9 %copy-start.5 = (pred[1024,1024]{0,1:T(8,128)(4,1)S(1)}, pred[1024,1024]{0,1:T(8,128)(4,1)}, u32[]{:S(2)}) copy-start(pred[1024,1024]{0,1:T(8,128)(4,1)} %copy-done.4) | copy-start | bytes 3145732
  245.4 6.9 %copy-start.26 = (bf16[1024,2,64]{0,2,1:T(8,128)(2,1)S(1)}, bf16[1024,2,64]{0,2,1:T(8,128)(2,1)}, u32[]{:S(2)}) copy-start(bf16[1024,2,64]{0,2,1:T(8,128)(2,1)} %squeeze.49) | copy-start | bytes 786436
  252.3 5.6 copy-start.18
  257.9 1.4 copy-start.16
  274.2 17.8 %all-to-all-start.3 = ((bf16[3,1024,1,128]{3,0,2,1:T(4,128)(2,1)}), bf16[3,1024,1,128]{3,0,2,1:T(4,128)(2,1)}, u32[]{:S(2)}, u32[]{:S(2)}) async-start(bf16[3,1024,1,128]{3,0,2,1:T(4,128)(2,1)} %pad_maximum_fusion.2), calls=%async_computation.3 | async-start | bytes 2097152 | tf_op jit(solution)/shard_map/all_to_all | solution.py:225
  278.5 127.2 %reduce-scatter.3.cloned.1.call-start = ((), (), s32[]{:S(2)}) async-start(), calls=%async_computation.8 | async-start | bytes 4734976 | tf_op jit(solution)/shard_map/reduce_scatter | solution.py:237
  294.6 3.2 copy-start.20
  294.6 4.7 copy-start.27
  294.6 4.7 copy-start.29
  294.6 4.7 copy-start.31
  297.7 4.4 copy-start.10
  297.7 4.4 collective-permute-start.3
  302.2 0.8 copy-start.12
  307.1 1.1 copy-start.7
  307.1 270.1 %reduce-scatter.5.cloned.1.call-start = ((), (), s32[]{:S(2)}) async-start(), calls=%async_computation.10 | async-start | bytes 9191424 | tf_op jit(solution)/shard_map/reduce_scatter | solution.py:193
  308.2 2.2 copy-start.22
  308.2 2.2 copy-start.24
  316.0 261.3 %copy-start.11 = (bf16[256,1024]{1,0:T(8,128)(2,1)S(1)}, bf16[256,1024]{1,0:T(8,128)(2,1)}, u32[]{:S(2)}) copy-start(bf16[256,1024]{1,0:T(8,128)(2,1)} %copy-done.10) | copy-start | bytes 1572868
  316.0 261.3 %copy-start.13 = (bf16[256,1024]{1,0:T(8,128)(2,1)S(1)}, bf16[256,1024]{1,0:T(8,128)(2,1)}, u32[]{:S(2)}) copy-start(bf16[256,1024]{1,0:T(8,128)(2,1)} %copy-done.12) | copy-start | bytes 1572868
  316.0 288.9 %all-gather.9.cloned.1.call-start = ((), (), s32[]{:S(2)}) async-start(), calls=%async_computation.9 | async-start | bytes 1392640 | tf_op jit(solution)/shard_map/all_gather | solution.py:246
  405.7 236.7 %all-gather.11.cloned.1.call-start = ((), (), s32[]{:S(2)}) async-start(), calls=%async_computation.11 | async-start | bytes 2703360 | tf_op jit(solution)/shard_map/all_gather | solution.py:245
  646.7 3.7 copy-start.1
Sparse Core Ops, SparseCore 0:
  13.8 80.3 all-gather.4
  97.6 120.5 all-gather.6
  307.2 98.4 reduce-scatter.2
  411.2 165.9 reduce-scatter.4
  578.9 26.0 all-gather.8
  606.6 35.7 all-gather.10

commit v3 on v2

--- a/solution.py
+++ b/solution.py
@@ -234,14 +234,11 @@
     gain_grads = jnp.pad(
         jnp.stack([grad_gain_attn, grad_gain_mlp], axis=1), ((0, 0), (0, LANES - 2))
     )
-    share_attn = lax.psum_scatter(
-        jnp.concatenate(
-            [grad_qkv.astype(bf16), grad_attn_out.astype(bf16), gain_grads.astype(bf16)], axis=1
-        ),
-        BOTH,
-        scatter_dimension=0,
-        tiled=True,
-    )
+    attn_grads = jnp.concatenate(
+        [grad_qkv.astype(bf16), grad_attn_out.astype(bf16), gain_grads.astype(bf16)], axis=1
+    )
+    attn_grads, share_mlp = lax.optimization_barrier((attn_grads, share_mlp))
+    share_attn = lax.psum_scatter(attn_grads, BOTH, scatter_dimension=0, tiled=True)
     own_mlp = lax.all_gather(share_mlp, "ctx", axis=0, tiled=True)
     own_attn = lax.all_gather(share_attn, "ctx", axis=0, tiled=True)
     own_in = jnp.stack([own_mlp[:, :units], own_mlp[:, padded : padded + units]]).astype(f32)

time: 667 us -> 596 us (0.89)
  waiting for transfers between devices: 499 us -> 430 us
  matrix products: 46.7 us -> 53.8 us
    reduce_scatter x1, waiting for transfers between devices: 171 us -> 84.2 us  [local(): lax.psum_scatter(jnp.concatenate([grad_in.astype(bf16), grad_mlp_out.asty...]
    reduce_scatter x1, waiting for transfers between devices: 89.6 us -> 101 us  [local(): lax.psum_scatter(attn_grads, BOTH, scatter_dimension=0, tiled=True)]
  transfers between devices with their start and end apart: 13 -> 13, of which waited for: 12 -> 11; matrix products, arithmetic and copies ran while one was open for 7% -> 16% of each run, Pallas kernels for 0% -> 0%
where the time goes in v3:
time: 596 us; the launch traced here: 587 us
  waiting for transfers between devices  430 us (72%)
  matrix products  53.8 us (9%)
  other arithmetic  33.8 us (6%)
  local copies, waits for them, and re-layouts  30.4 us (5%)
  between operations  15.4 us (3%)
  starting transfers between devices  12.5 us (2%)
  blocking collectives  11 us (2%)
    reduce_scatter x1, waiting for transfers between devices, local(): lax.psum_scatter(attn_grads, BOTH, scatter_dimension=0, tiled=True)  101 us
    reduce_scatter x1, waiting for transfers between devices, local(): lax.psum_scatter(jnp.concatenate([grad_in.astype(bf16), grad_mlp_out.asty...  84.2 us
    all_gather x1, waiting for transfers between devices, local(): attn_all = lax.all_gather(attn_block, BOTH, axis=0, tiled=True)  78.4 us
    all_gather x1, waiting for transfers between devices, local(): mlp_all = lax.all_gather(mlp_block, BOTH, axis=0, tiled=True)  69.1 us
    all_gather x1, waiting for transfers between devices, local(): own_mlp = lax.all_gather(share_mlp, 'ctx', axis=0, tiled=True)  35.9 us
    all_gather x1, waiting for transfers between devices, local(): own_attn = lax.all_gather(share_attn, 'ctx', axis=0, tiled=True)  20.8 us
    all_to_all x1, waiting for transfers between devices, local(): lax.all_to_all(grad_stack, 'ctx', split_axis=1, concat_axis=2, tiled=True)  17.6 us
  transfers between devices with their start and end apart: 13, of which 11 were waited for; matrix products, arithmetic and copies ran while one was open for 16% of the time, Pallas kernels for 0%

profile of v3, /device:TPU:0, one launch (start us, length us, event | category | flops | bytes accessed | tf_op | source)
XLA Modules:
  0.0 586.6 jit_solution(6529585446617144346)
XLA Ops:
  8.9 1.1 copy.153
  10.0 1.0 bitcast_dynamic-update-slice_fusion.3
  10.9 1.0 bitcast_dynamic-update-slice_fusion.2
  11.9 1.0 bitcast_dynamic-update-slice_fusion.1
  15.0 0.8 pad_maximum_fusion.7
  15.8 78.4 %all-gather.5.cloned.1.call-done = bf16[1024,2176]{1,0:T(8,128)(2,1)} async-done(((bf16[64,2176]{1,0:T(8,128)(2,1)}), bf16[1024,2176]{1,0:T(8,128)(2,1)}) %all-gather.5.cloned.1.call-update) | async-done | bytes 4456464 | tf_op jit(solution)/shard_map/all_gather | solution.py:134
  95.1 1.3 convert_reduce_fusion.1
  96.4 3.0 fusion.18
  99.8 1.0 pad_maximum_fusion.5
  100.8 3.5 all-to-all-start
  104.5 1.0 fusion.74
  106.1 11.4 %all-to-all-done = bf16[3,256,4,128]{3,1,0,2:T(8,128)(2,1)S(1)} async-done(((bf16[3,256,4,128]{3,1,0,2:T(8,128)(2,1)}), bf16[3,256,4,128]{3,1,0,2:T(8,128)(2,1)S(1)}, u32[]{:S(2)}, u32[]{:S(2)}) %all-to-all-start) | async-done | bytes 786464 | tf_op jit(solution)/shard_map/all_to_all | solution.py:159
  117.5 1.1 slice_convert_fusion
  118.6 1.3 copy.160
  120.4 0.9 squeeze.49
  121.2 2.0 copy.159
  123.3 1.3 reshape.240
  125.0 1.9 fusion.8
  126.9 2.0 fusion.1
  128.9 2.8 fusion.45
  133.4 11.0 %all_to_all.60 = bf16[4,2,16384]{2,1,0:T(2,128)(2,1)S(1)} all-to-all(bf16[4,2,16384]{2,1,0:T(2,128)(2,1)S(1)} %reshape.247), channel_id=1, replica_groups=mesh['dp'=4,'ctx'=4,'tensor'=2] {'ctx'}, dimensions={0} | all-to-all | bytes 524288 | tf_op jit(solution)/shard_map/all_to_all | solution.py:165
  144.9 1.8 convolution_convert_fusion.4
  146.8 1.9 collective-permute-done
  149.2 69.1 %all-gather.7.cloned.1.call-done = bf16[1024,4224]{1,0:T(8,128)(2,1)} async-done(((bf16[64,4224]{1,0:T(8,128)(2,1)}), bf16[1024,4224]{1,0:T(8,128)(2,1)}) %all-gather.7.cloned.1.call-update) | async-done | bytes 8650768 | tf_op jit(solution)/shard_map/all_gather | solution.py:139
  218.3 4.4 fusion.5
  222.7 3.2 fusion.29
  225.9 1.0 fusion.13
  227.0 1.8 convolution_convert_fusion
  228.9 3.7 pad_maximum_fusion
  232.6 4.8 fusion.36
  237.5 3.2 fusion.33
  241.8 1.0 collective-permute-done.1
  242.8 1.3 multiply_add_fusion
  244.1 2.5 convolution_convert_fusion.5
  246.5 1.8 copy.192
  248.3 4.3 all-to-all-start.2
  252.6 8.1 %all-to-all-done.2 = bf16[256,4,128]{0,2,1:T(8,128)(2,1)} async-done(((bf16[256,4,128]{0,2,1:T(8,128)(2,1)}), bf16[256,4,128]{0,2,1:T(8,128)(2,1)}, u32[]{:S(2)}, u32[]{:S(2)}) %all-to-all-start.2) | async-done | bytes 262176 | tf_op jit(solution)/shard_map/all_to_all | solution.py:209
  260.7 1.9 copy.166
  262.6 1.8 reshape.238
  264.4 6.8 %fusion.46 = bf16[2,64,1024]{2,1,0:T(8,128)(2,1)} fusion(bf16[1024,2,64]{0,2,1:T(8,128)(2,1)} %reshape.238, f32[2,1024,1024]{1,2,0:T(8,128)} %copy-done.3, f32[2,1024]{1,0:T(2,128)S(1)} %log_add_fusion, pred[1024,1024]{0,1:T(8,128)(4,1)S(1)} %copy-done.5), kind=kOutput, calls=%fused_computation.64 | convolution fusion | flops 276955136 | bytes 9969664 | tf_op jit(solution)/shard_map/hbc,bhe->che/dot_general | solution.py:91
  271.2 2.0 copy.173
  273.2 1.1 multiply_reduce_fusion.3
  274.3 6.9 %multiply_convert_fusion = bf16[2,1024,1024]{1,2,0:T(8,128)(2,1)S(1)} fusion(f32[2,1024,1024]{1,2,0:T(8,128)} %copy-done.3, f32[2,1024]{1,0:T(2,128)S(1)} %bitcast.117, f32[2,1024]{1,0:T(2,128)S(1)} %log_add_fusion, pred[1024,1024]{0,1:T(8,128)(4,1)S(1)} %copy-done.5, bf16[1024,2,64]{0,2,1:T(8,128)(2,1)} %reshape.238, bf16[1024,2,64]{0,2,1:T(8,128)(2,1)} %squeeze.49), kind=kOutput, calls=%fused_computation.3 | convolution fusion | flops 283115520 | bytes 14172160 | tf_op jit(solution)/shard_map/bhe,che->hbc/dot_general | solution.py:92
  281.2 1.4 convolution_bitcast_fusion.1
  282.6 0.9 broadcast_multiply_fusion.1
  284.6 2.8 pad_maximum_fusion.2
  287.4 3.5 all-to-all-start.3
  291.3 17.6 %all-to-all-done.3 = bf16[3,1024,1,128]{3,0,2,1:T(4,128)(2,1)S(1)} async-done(((bf16[3,1024,1,128]{3,0,2,1:T(4,128)(2,1)}), bf16[3,1024,1,128]{3,0,2,1:T(4,128)(2,1)S(1)}, u32[]{:S(2)}, u32[]{:S(2)}) %all-to-all-start.3) | async-done | bytes 786464 | tf_op jit(solution)/shard_map/all_to_all | solution.py:225
  309.5 3.1 fusion.30
  313.2 3.9 convolution_convert_fusion.2
  318.7 3.7 fusion.7
  322.4 84.2 %reduce-scatter.3.cloned.1.call-done = bf16[64,4224]{1,0:T(8,128)(2,1)} async-done(((bf16[1024,4224]{1,0:T(8,128)(2,1)}), bf16[64,4224]{1,0:T(8,128)(2,1)}) %reduce-scatter.3.cloned.1.call-update) | async-done | bytes 540688 | tf_op jit(solution)/shard_map/reduce_scatter | solution.py:193
  407.3 100.6 %reduce-scatter.5.cloned.1.call-done = bf16[64,2176]{1,0:T(8,128)(2,1)} async-done(((bf16[1024,2176]{1,0:T(8,128)(2,1)}), bf16[64,2176]{1,0:T(8,128)(2,1)}) %reduce-scatter.5.cloned.1.call-update) | async-done | bytes 278544 | tf_op jit(solution)/shard_map/reduce_scatter | solution.py:241
  508.0 1.4 fusion.56
  509.4 35.9 %all-gather.11.cloned.1.call-done = bf16[256,4224]{1,0:T(8,128)(2,1)} async-done(((bf16[64,4224]{1,0:T(8,128)(2,1)}), bf16[256,4224]{1,0:T(8,128)(2,1)}) %all-gather.11.cloned.1.call-update) | async-done | bytes 2162704 | tf_op jit(solution)/shard_map/all_gather | solution.py:242
  545.3 2.8 convert_bitcast_fusion
  548.1 1.5 copy.183
  549.6 1.5 maximum_convert_fusion
  551.1 2.1 copy.182
  553.3 20.8 %all-gather.9.cloned.1.call-done = bf16[256,2176]{1,0:T(8,128)(2,1)} async-done(((bf16[64,2176]{1,0:T(8,128)(2,1)}), bf16[256,2176]{1,0:T(8,128)(2,1)}) %all-gather.9.cloned.1.call-update) | async-done | bytes 1114128 | tf_op jit(solution)/shard_map/all_gather | solution.py:243
  574.0 0.8 convert_bitcast_fusion.2
  575.7 1.3 convert_bitcast_fusion.1
  577.0 1.0 copy.181
  578.0 1.3 maximum_convert_fusion.1
  (137 shorter events, 16.0 us)
Async XLA Ops:
  7.2 6.6 %copy-start = (bf16[1312,256]{1,0:T(8,128)(2,1)S(1)}, bf16[1312,256]{1,0:T(8,128)(2,1)}, u32[]{:S(2)}) copy-start(bf16[1312,256]{1,0:T(8,128)(2,1)} %param.16) | copy-start | bytes 2015236
  7.2 6.9 %copy-start.11 = (bf16[2,256,1312]{1,2,0:T(8,128)(2,1)S(1)}, bf16[2,256,1312]{1,2,0:T(8,128)(2,1)}, u32[]{:S(2)}) copy-start(bf16[2,256,1312]{1,2,0:T(8,128)(2,1)} %param.15) | copy-start | bytes 4030468
  7.2 87.0 %all-gather.5.cloned.1.call-start = ((), (), s32[]{:S(2)}) async-start(), calls=%async_computation.6 | async-start | bytes 4734976 | tf_op jit(solution)/shard_map/all_gather | solution.py:134
  13.7 204.6 %all-gather.7.cloned.1.call-start = ((), (), s32[]{:S(2)}) async-start(), calls=%async_computation.7 | async-start | bytes 9191424 | tf_op jit(solution)/shard_map/all_gather | solution.py:139
  14.2 80.0 %copy-start.22 = (s32[1,8]{1,0:T(1,128)S(1)}, s32[1,8]{1,0:T(1,128)}, u32[]{:S(2)}) copy-start(s32[1,8]{1,0:T(1,128)} %param.10) | copy-start | bytes 100
  14.2 80.4 %copy-start.2 = (bf16[256,1024]{1,0:T(8,128)(2,1)S(1)}, bf16[256,1024]{1,0:T(8,128)(2,1)}, u32[]{:S(2)}) copy-start(bf16[256,1024]{1,0:T(8,128)(2,1)} %param.9) | copy-start | bytes 1572868
  100.8 16.7 %all-to-all-start = ((bf16[3,256,4,128]{3,1,0,2:T(8,128)(2,1)}), bf16[3,256,4,128]{3,1,0,2:T(8,128)(2,1)S(1)}, u32[]{:S(2)}, u32[]{:S(2)}) async-start(bf16[3,256,4,128]{3,1,0,2:T(8,128)(2,1)} %pad_maximum_fusion.5), calls=%async_computation | async-start | bytes 1572864 | tf_op jit(solution)/shard_map/all_to_all | solution.py:159
  104.3 302.3 %reduce-scatter.3.cloned.1.call-start = ((), (), s32[]{:S(2)}) async-start(), calls=%async_computation.8 | async-start | bytes 9191424 | tf_op jit(solution)/shard_map/reduce_scatter | solution.py:193
  106.1 22.8 %copy-start.4 = (pred[1024,1024]{0,1:T(8,128)(4,1)}, pred[1024,1024]{0,1:T(8,128)(4,1)S(1)}, u32[]{:S(2)}) copy-start(pred[1024,1024]{0,1:T(8,128)(4,1)S(1)} %broadcast_compare_fusion) | copy-start | bytes 3145732
  125.0 1.9 copy-start.12
  126.9 4.9 copy-start.3
  126.9 2.0 copy-start.19
  131.8 1.6 copy-start.16
  144.9 1.9 copy-start.14
  146.7 2.0 collective-permute-start
  218.3 4.4 copy-start.6
  225.9 1.1 copy-start.17
  225.9 1.1 copy-start.18
  237.4 5.4 copy-start.7
  237.4 3.8 collective-permute-start.2
  240.7 2.1 collective-permute-start.1
  244.1 20.4 %copy-start.5 = (pred[1024,1024]{0,1:T(8,128)(4,1)S(1)}, pred[1024,1024]{0,1:T(8,128)(4,1)}, u32[]{:S(2)}) copy-start(pred[1024,1024]{0,1:T(8,128)(4,1)} %copy-done.4) | copy-start | bytes 3145732
  248.3 12.4 %all-to-all-start.2 = ((bf16[256,4,128]{0,2,1:T(8,128)(2,1)}), bf16[256,4,128]{0,2,1:T(8,128)(2,1)}, u32[]{:S(2)}, u32[]{:S(2)}) async-start(bf16[256,4,128]{0,2,1:T(8,128)(2,1)} %bitcast.106), calls=%async_computation.2 | async-start | bytes 524288 | tf_op jit(solution)/shard_map/all_to_all | solution.py:209
  274.3 6.9 %copy-start.13 = (bf16[1024,2,64]{0,2,1:T(8,128)(2,1)S(1)}, bf16[1024,2,64]{0,2,1:T(8,128)(2,1)}, u32[]{:S(2)}) copy-start(bf16[1024,2,64]{0,2,1:T(8,128)(2,1)} %copy-done.12) | copy-start | bytes 786436
  283.5 1.1 copy-start.10
  287.4 21.5 %all-to-all-start.3 = ((bf16[3,1024,1,128]{3,0,2,1:T(4,128)(2,1)}), bf16[3,1024,1,128]{3,0,2,1:T(4,128)(2,1)S(1)}, u32[]{:S(2)}, u32[]{:S(2)}) async-start(bf16[3,1024,1,128]{3,0,2,1:T(4,128)(2,1)} %pad_maximum_fusion.2), calls=%async_computation.3 | async-start | bytes 2097152 | tf_op jit(solution)/shard_map/all_to_all | solution.py:225
  290.9 217.0 %reduce-scatter.5.cloned.1.call-start = ((), (), s32[]{:S(2)}) async-start(), calls=%async_computation.9 | async-start | bytes 4734976 | tf_op jit(solution)/shard_map/reduce_scatter | solution.py:241
  309.4 3.3 copy-start.20
  309.5 3.1 copy-start.21
  309.5 3.2 copy-start.15
  312.6 4.5 collective-permute-start.3
  317.1 0.8 copy-start.8
  322.4 185.6 %copy-start.9 = (bf16[256,1024]{1,0:T(8,128)(2,1)S(1)}, bf16[256,1024]{1,0:T(8,128)(2,1)}, u32[]{:S(2)}) copy-start(bf16[256,1024]{1,0:T(8,128)(2,1)} %copy-done.8) | copy-start | bytes 1572868
  406.7 138.6 %all-gather.11.cloned.1.call-start = ((), (), s32[]{:S(2)}) async-start(), calls=%async_computation.11 | async-start | bytes 2703360 | tf_op jit(solution)/shard_map/all_gather | solution.py:242
  407.3 166.8 %all-gather.9.cloned.1.call-start = ((), (), s32[]{:S(2)}) async-start(), calls=%async_computation.10 | async-start | bytes 1392640 | tf_op jit(solution)/shard_map/all_gather | solution.py:243
  551.1 28.2 %copy-start.1 = (bf16[1312,256]{1,0:T(8,128)(2,1)S(1)}, bf16[1312,256]{1,0:T(8,128)(2,1)}, u32[]{:S(2)}) copy-start(bf16[1312,256]{1,0:T(8,128)(2,1)} %param.16) | copy-start | bytes 2015236
Sparse Core Ops, SparseCore 0:
  13.8 80.3 all-gather.4
  97.6 120.6 all-gather.6
  232.7 173.8 reduce-scatter.2
  408.8 99.0 reduce-scatter.4
  509.6 35.6 all-gather.10
  547.0 27.0 all-gather.8
